TPU v7x, 32 devices: a whole 2x2x4 slice. The times are simulated.
32 devices in a mesh: dp: 8 (over z, core), mp: 4 (over y, x).
Axes of the slice: x: 2, y: 2, z: 4, core: 2. Of those that a mesh axis runs over, the one named last changes fastest.
Arguments:
- tokens: bfloat16 [2048, 3072], P('dp'), may hold values from -60 to 60
- ln_gain: float32 [3072], replicated, may hold values from 0.25 to 1.75
- q_weight: bfloat16 [3072, 4096], P('dp', 'mp'), may hold values from -1 to 1
- k_weight: bfloat16 [3072, 4096], P('dp', 'mp'), may hold values from -1 to 1
- v_weight: bfloat16 [3072, 4096], P('dp', 'mp'), may hold values from -0.109375 to 0.109375
- q_gain: float32 [4096], P('mp'), may hold values from 0.6 to 6
- k_gain: float32 [4096], P('mp'), may hold values from 0.6 to 6
- out_weight: bfloat16 [3072, 4096], P('dp', 'mp'), may hold values from -0.25 to 0.25
Outputs:
- mixed: bfloat16 [2048, 3072], P(('dp', 'mp'))
All inputs are finite; a program needn't handle non-finite values.
Results may differ from a plain program's by a relative error of at most 0.018.
Values may be sent and summed in bfloat16 or wider, within the bound.
A program may use at most 128 MiB of HBM per device.

v0:
```python
import functools
import math

import jax
import jax.numpy as jnp
from jax import lax
from jax.experimental import pallas as pl
from jax.experimental.pallas import tpu as pltpu
from jax.sharding import PartitionSpec as P

HEAD_DIM = 128
IMG_TOKENS = 256


epsilon = 1e-06


def layer_norm(values, scale_gain):
    average = jnp.mean(values, axis=-1, keepdims=True)
    centred = values - average
    variance = jnp.mean(centred * centred, axis=-1, keepdims=True)
    return centred * lax.rsqrt(variance + epsilon) * scale_gain


def head_norm(projected, scale_gain):
    heads_count = projected.shape[1] // HEAD_DIM
    shaped = projected.reshape(projected.shape[0], heads_count, HEAD_DIM)
    normed = layer_norm(shaped, scale_gain.reshape(heads_count, HEAD_DIM))
    return normed.reshape(projected.shape).astype(jnp.bfloat16)


def attend(queries, key_rows, value_rows):
    scores = jnp.einsum(
        "bqhd,bkhd->bhqk", queries, key_rows, preferred_element_type=jnp.float32
    ) * (1.0 / math.sqrt(HEAD_DIM))
    highest = jnp.max(scores, axis=-1, keepdims=True)
    weights = jnp.exp(scores - highest)
    probs = (weights / jnp.sum(weights, axis=-1, keepdims=True)).astype(jnp.bfloat16)
    context = jnp.einsum("bhqk,bkhd->bqhd", probs, value_rows, preferred_element_type=jnp.float32)
    return context.astype(jnp.bfloat16)


def place_three(holder, pieces, offset, local_width):
    holder = lax.dynamic_update_slice(holder, pieces[0], (offset, 0))
    holder = lax.dynamic_update_slice(holder, pieces[1], (offset, local_width))
    return lax.dynamic_update_slice(holder, pieces[2], (offset, 2 * local_width))


def gathered_weights(tokens, ln_gain, q_weight, k_weight, v_weight, q_gain, k_gain, out_weight):
    normed = layer_norm(tokens.astype(jnp.float32), ln_gain).astype(jnp.bfloat16)
    token_count = normed.shape[0]
    local_width = q_weight.shape[1]
    feature_count = normed.shape[1]
    stacked = jnp.zeros((feature_count, 3 * local_width), jnp.bfloat16)
    projections = place_three(
        stacked,
        (
            lax.all_gather(q_weight, "dp", axis=0, tiled=True),
            lax.all_gather(k_weight, "dp", axis=0, tiled=True),
            lax.all_gather(v_weight, "dp", axis=0, tiled=True),
        ),
        jnp.int32(0),
        local_width,
    )
    combined = jnp.dot(normed, projections, preferred_element_type=jnp.float32)
    queries = combined[:, :local_width]
    key_rows = combined[:, local_width : 2 * local_width]
    value_cast = combined[:, 2 * local_width :].astype(jnp.bfloat16)
    query_normed = head_norm(queries, q_gain)
    key_normed = head_norm(key_rows, k_gain)
    images = token_count // IMG_TOKENS
    shaped = (images, IMG_TOKENS, local_width // HEAD_DIM, HEAD_DIM)
    context = attend(
        query_normed.reshape(shaped), key_normed.reshape(shaped), value_cast.reshape(shaped)
    )
    context = context.reshape(token_count, local_width)
    out_full = lax.all_gather(out_weight, "dp", axis=0, tiled=True)
    return lax.psum_scatter(
        lax.dot_general(
            context, out_full, (((1,), (1,)), ((), ())), preferred_element_type=jnp.float32
        ).astype(jnp.bfloat16),
        "mp",
        scatter_dimension=0,
        tiled=True,
    )


MESH = pl.DeviceIdType.MESH


def exchange_kernel(
    pairs, groups, tokens, ln_gain, q_w, k_w, v_w, q_gain, k_gain, out_w, result,
    raw, normed, weights, out_rows, context, partial, arrived, summed, final,
    local_sem, up_send, down_send, token_recv, peer_send, peer_recv,
    w_send, w_recv, own_send, own_recv, pass_send, pass_recv, out_send, out_recv,
    c_up, c_down, c_recv, p_send, p_recv, f_send, f_recv,
):
    dp = lax.axis_index("dp")
    group = lax.axis_index("mp")
    pair = dp // 2
    core = dp % 2
    rows = tokens.shape[0]
    part = rows // groups
    shard = q_w.shape[0]
    width = q_w.shape[1] // pairs
    span = 2 * shard
    heads = width // HEAD_DIM

    def at_pair(other):
        return (other * 2 + core, group)

    partner = (pair * 2 + (1 - core), group)

    def at_group(other):
        return (dp, other)

    def remote(source, target, send, recv, device):
        return pltpu.make_async_remote_copy(
            src_ref=source, dst_ref=target, send_sem=send, recv_sem=recv,
            device_id=device, device_id_type=MESH,
        )

    greeted = pltpu.get_barrier_semaphore()
    for step in range(1, pairs):
        pl.semaphore_signal(
            greeted, inc=1, device_id=at_pair((pair + step) % pairs), device_id_type=MESH
        )
    for step in range(1, groups):
        pl.semaphore_signal(
            greeted, inc=1, device_id=at_group((group + step) % groups), device_id_type=MESH
        )
    pl.semaphore_signal(greeted, inc=1, device_id=partner, device_id_type=MESH)

    projections = (q_w, k_w, v_w)

    def columns(other, h, t):
        start = pl.multiple_of(other * width + h * HEAD_DIM, HEAD_DIM)
        return projections[t].at[:, pl.ds(start, HEAD_DIM)]

    def slot(h, block, side, t):
        return weights.at[h, block, side, :, pl.ds(t * HEAD_DIM, HEAD_DIM)]

    quarter = pl.ds(pl.multiple_of(group * part, part), part)
    locals_ = [pltpu.make_async_copy(tokens, raw.at[pair], local_sem.at[0])]
    locals_.append(pltpu.make_async_copy(out_w, out_rows.at[core], local_sem.at[1]))
    for h in range(heads):
        for t in range(3):
            locals_.append(
                pltpu.make_async_copy(
                    columns(pair, h, t), slot(h, pair, core, t), local_sem.at[2 + 3 * h + t]
                )
            )
    for copy in locals_:
        copy.start()
    pl.semaphore_wait(greeted, pairs + groups - 1)

    def first_hop(up):
        return remote(
            tokens.at[quarter, :], raw.at[pair, quarter, :],
            (up_send if up else down_send).at[pair], token_recv.at[pair],
            at_pair(pair + 1 if up else pair - 1),
        )

    def next_hop(block, up):
        return remote(
            raw.at[block, quarter, :], raw.at[block, quarter, :],
            (up_send if up else down_send).at[block], token_recv.at[block],
            at_pair(pair + 1 if up else pair - 1),
        )

    beside = group + 1 - 2 * (group % 2)
    across = (group + 2) % 4
    first = jnp.where(core == 0, beside, across)
    second = jnp.where(core == 0, across, beside)
    opposite = 3 - group

    def part_of(block, other):
        return raw.at[block, pl.ds(pl.multiple_of(other * part, part), part), :]

    def peer_copy(block, owner, place, other):
        there = part_of(block, owner)
        return remote(
            there, there, peer_send.at[block, place], peer_recv.at[block, owner], at_group(other)
        )

    def to_first(block):
        return peer_copy(block, group, 0, first)

    def to_second(block):
        return peer_copy(block, group, 1, second)

    def cross(block):
        return peer_copy(block, first, 2, second)

    def from_peer(block, owner):
        return peer_copy(block, owner, 0, first)

    def weight_to(other, h, t):
        return remote(
            columns(other, h, t), slot(h, pair, core, t),
            w_send.at[other, h, t], w_recv.at[pair, h, t], at_pair(other),
        )

    def weight_from(other, h, t):
        there = slot(h, other, core, t)
        return remote(there, there, w_send.at[other, h, t], w_recv.at[other, h, t], at_pair(other))

    def own_weight(h, t):
        return remote(
            columns(pair, h, t), slot(h, pair, core, t), own_send.at[h, t], own_recv.at[h, t], partner
        )

    def partner_weight(h, t):
        there = slot(h, pair, 1 - core, t)
        return remote(there, there, own_send.at[h, t], own_recv.at[h, t], partner)

    def pass_on(other, h):
        there = weights.at[h, other, core]
        return remote(there, there, pass_send.at[other, h], pass_recv.at[other, h], partner)

    def passed(other, h):
        there = weights.at[h, other, 1 - core]
        return remote(there, there, pass_send.at[other, h], pass_recv.at[other, h], partner)

    def out_over():
        return remote(out_w, out_rows.at[core], out_send, out_recv, partner)

    def out_back():
        there = out_rows.at[1 - core]
        return remote(there, there, out_send, out_recv, partner)

    has_up = pair + 1 < pairs
    has_down = pair > 0

    @pl.when(has_up)
    def _():
        first_hop(True).start()

    @pl.when(has_down)
    def _():
        first_hop(False).start()

    def send_weights(up, some):
        for h in some:
            for distance in range(pairs - 1, 0, -1) if h == 0 else range(1, pairs):
                other = pair + distance if up else pair - distance

                @pl.when(other < pairs if up else other >= 0)
                def _():
                    for t in range(3):
                        weight_to(other, h, t).start()

    @pl.when(pair == 0)
    def _():
        send_weights(True, range(1))

    @pl.when(pair == pairs - 1)
    def _():
        send_weights(False, range(1))

    for h in range(heads):
        for t in range(3):
            own_weight(h, t).start()

    def normalise(block):
        @pl.loop(0, rows // 16)
        def _(chunk):
            place = pl.ds(pl.multiple_of(chunk * 16, 16), 16)
            values = raw[block, place, :].astype(jnp.float32)
            average = jnp.mean(values, axis=-1, keepdims=True)
            centred = values - average
            variance = jnp.mean(centred * centred, axis=-1, keepdims=True)
            scaled = centred * lax.rsqrt(variance + epsilon) * ln_gain[...]
            scaled = scaled.astype(jnp.bfloat16)
            for p in range(pairs):
                normed[p, block, place, :] = scaled[:, p * span : (p + 1) * span]

    for copy in locals_:
        copy.wait()
    normalise(pair)

    def relay(block, up):
        next_hop(block, up).wait_recv()

        @pl.when(has_up if up else has_down)
        def _():
            next_hop(block, up).start()

        to_first(block).start()
        to_second(block).start()

    for distance in range(1, pairs):
        @pl.when(pair - distance >= 0)
        def _():
            relay(pair - distance, True)

        @pl.when(pair + distance < pairs)
        def _():
            relay(pair + distance, False)

        @pl.when(has_up & (pair == distance))
        def _():
            send_weights(True, range(1))

        @pl.when(has_down & (pair == pairs - 1 - distance))
        def _():
            send_weights(False, range(1))

    def cross_tokens(block):
        from_peer(block, first).wait_recv()
        cross(block).start()

    for distance in range(1, pairs):
        @pl.when(pair - distance >= 0)
        def _():
            cross_tokens(pair - distance)

        @pl.when(pair + distance < pairs)
        def _():
            cross_tokens(pair + distance)

        if distance == min(2, pairs - 1):
            send_weights(True, range(1, heads))
            send_weights(False, range(1, heads))


    out_over().start()

    def take_tokens(block):
        from_peer(block, second).wait_recv()
        from_peer(block, opposite).wait_recv()
        normalise(block)

    def pass_weights(h):
        @pl.loop(1, pairs)
        def _(k):
            block = (pair + k) % pairs
            for t in range(3):
                weight_from(block, h, t).wait_recv()
            pass_on(block, h).start()

    for distance in range(1, pairs):
        if distance == pairs - 1:
            pass_weights(0)

        @pl.when(pair - distance >= 0)
        def _():
            take_tokens(pair - distance)

        @pl.when(pair + distance < pairs)
        def _():
            take_tokens(pair + distance)

    def head_layer_norm(values, scale_gain):
        average = jnp.mean(values, axis=-1, keepdims=True)
        centred = values - average
        variance = jnp.mean(centred * centred, axis=-1, keepdims=True)
        return (centred * lax.rsqrt(variance + epsilon) * scale_gain).astype(jnp.bfloat16)

    def context_hop(block, image, h, up):
        there = context.at[block, image, :, pl.ds(h * HEAD_DIM, HEAD_DIM)]
        return remote(
            there, there,
            (c_up if up else c_down).at[block, image, h], c_recv.at[block, image, h],
            at_pair(pair + 1 if up else pair - 1),
        )

    def pass_context(image, h, distance):
        for up in (True, False):
            block = pair - distance if up else pair + distance

            @pl.when(block >= 0 if up else block < pairs)
            def _():
                context_hop(block, image, h, up).wait_recv()

                @pl.when(has_up if up else has_down)
                def _():
                    context_hop(block, image, h, up).start()

    for h in range(heads):
        if h > 0:
            pass_weights(h)
        for t in range(3):
            partner_weight(h, t).wait_recv()

        @pl.loop(1, pairs)
        def _(k):
            passed((pair + k) % pairs, h).wait_recv()

        lanes = slice(h * HEAD_DIM, (h + 1) * HEAD_DIM)

        @pl.loop(0, pairs)
        def _(image):
            total = None
            for p in range(pairs):
                product = jnp.dot(
                    normed[p, image], weights[h, p].reshape(span, 3 * HEAD_DIM),
                    preferred_element_type=jnp.float32,
                )
                total = product if total is None else total + product
            queries = head_layer_norm(total[:, :HEAD_DIM], q_gain[pair, :, lanes])
            key_rows = head_layer_norm(total[:, HEAD_DIM : 2 * HEAD_DIM], k_gain[pair, :, lanes])
            value_rows = total[:, 2 * HEAD_DIM :].astype(jnp.bfloat16)
            scores = lax.dot_general(
                queries, key_rows, (((1,), (1,)), ((), ())), preferred_element_type=jnp.float32
            ) * (1.0 / math.sqrt(HEAD_DIM))
            highest = jnp.max(scores, axis=-1, keepdims=True)
            spread = jnp.exp(scores - highest)
            probs = (spread / jnp.sum(spread, axis=-1, keepdims=True)).astype(jnp.bfloat16)
            mixed = jnp.dot(probs, value_rows, preferred_element_type=jnp.float32)
            context[pair, image, :, lanes] = mixed.astype(jnp.bfloat16)

            @pl.when(has_up)
            def _():
                context_hop(pair, image, h, True).start()

            @pl.when(has_down)
            def _():
                context_hop(pair, image, h, False).start()

            if h > 0:
                pass_context(image, h - 1, 1)

    for distance in range(1, pairs):
        @pl.loop(0, pairs)
        def _(image):
            for h in range(heads):
                hop = distance + (1 if h < heads - 1 else 0)
                if hop < pairs and not (distance == pairs - 1 and h == heads - 1):
                    pass_context(image, h, hop)

    def partial_to(image, step):
        other = (group + step) % groups
        return remote(
            partial.at[image, pl.ds(pl.multiple_of(other * part, part), part), :],
            arrived.at[image, group],
            p_send.at[image, step - 1], p_recv.at[image, group], at_group(other),
        )

    def partial_from(image, step):
        other = (group + step) % groups
        there = arrived.at[image, other]
        return remote(there, there, p_send.at[image, step - 1], p_recv.at[image, other], at_group(other))

    out_back().wait_recv()

    @pl.loop(0, pairs)
    def _(image):
        pass_context(image, heads - 1, pairs - 1)

        for c in range(2):
            total = None
            for p in range(pairs):
                product = lax.dot_general(
                    context[p, image], out_rows[c, :, p * width : (p + 1) * width],
                    (((1,), (1,)), ((), ())), preferred_element_type=jnp.float32,
                )
                total = product if total is None else total + product
            partial[image, :, c * shard : (c + 1) * shard] = total.astype(jnp.bfloat16)
        for step in range(1, groups):
            partial_to(image, step).start()

    def final_to(image):
        return remote(
            summed.at[image], final.at[pair], f_send.at[image], f_recv.at[pair], at_pair(image)
        )

    def final_from(other):
        return remote(
            final.at[other], final.at[other], f_send.at[other], f_recv.at[other], at_pair(other)
        )

    @pl.loop(0, pairs)
    def _(image):
        total = partial[image, quarter, :].astype(jnp.float32)
        for step in range(1, groups):
            partial_from(image, step).wait_recv()
            total = total + arrived[image, (group + step) % groups].astype(jnp.float32)
        summed[image] = total.astype(jnp.bfloat16)

        @pl.when(image != pair)
        def _():
            final_to(image).start()

        @pl.when(image == pair)
        def _():
            final[pair] = summed[image]

    @pl.loop(1, pairs)
    def _(k):
        final_from((pair + k) % pairs).wait_recv()

    for p in range(pairs):
        result[:, p * span : (p + 1) * span] = final[p]

    @pl.when(has_up)
    def _():
        first_hop(True).wait_send()

    @pl.when(has_down)
    def _():
        first_hop(False).wait_send()

    for h in range(heads):
        for t in range(3):
            own_weight(h, t).wait_send()
    out_over().wait_send()
    for distance in range(1, pairs):
        for up in (True, False):
            inside = pair - distance >= 0 if up else pair + distance < pairs
            block = pair - distance if up else pair + distance

            @pl.when(inside & (has_up if up else has_down))
            def _():
                next_hop(block, up).wait_send()

                @pl.loop(0, pairs)
                def _(image):
                    for h in range(heads):
                        context_hop(block, image, h, up).wait_send()

    @pl.loop(0, pairs)
    def _(image):
        @pl.when(has_up)
        def _():
            for h in range(heads):
                context_hop(pair, image, h, True).wait_send()

        @pl.when(has_down)
        def _():
            for h in range(heads):
                context_hop(pair, image, h, False).wait_send()

        for step in range(1, groups):
            partial_to(image, step).wait_send()

    @pl.loop(1, pairs)
    def _(k):
        block = (pair + k) % pairs
        for h in range(heads):
            for t in range(3):
                weight_to(block, h, t).wait_send()
            pass_on(block, h).wait_send()
        to_first(block).wait_send()
        to_second(block).wait_send()
        cross(block).wait_send()
        final_to(block).wait_send()


def exchanged_heads(pairs, groups, tokens, ln_gain, q_w, k_w, v_w, q_gain, k_gain, out_w):
    rows, features = tokens.shape
    shard, local_width = q_w.shape
    width = local_width // pairs
    heads = width // HEAD_DIM
    part = rows // groups
    dma = pltpu.SemaphoreType.DMA
    in_hbm = pl.BlockSpec(memory_space=pl.ANY)
    in_vmem = pl.BlockSpec(memory_space=pltpu.VMEM)
    bf16 = jnp.bfloat16
    return pl.pallas_call(
        functools.partial(exchange_kernel, pairs, groups),
        out_shape=jax.ShapeDtypeStruct((part, features), bf16),
        in_specs=[in_hbm, in_vmem, in_hbm, in_hbm, in_hbm, in_vmem, in_vmem, in_hbm],
        out_specs=in_vmem,
        scratch_shapes=[
            pltpu.VMEM((pairs, rows, features), bf16),
            pltpu.VMEM((pairs, pairs, rows, 2 * shard), bf16),
            pltpu.VMEM((heads, pairs, 2, shard, 3 * HEAD_DIM), bf16),
            pltpu.VMEM((2, shard, local_width), bf16),
            pltpu.VMEM((pairs, pairs, rows, width), bf16),
            pltpu.VMEM((pairs, rows, 2 * shard), bf16),
            pltpu.VMEM((pairs, groups, part, 2 * shard), bf16),
            pltpu.VMEM((pairs, part, 2 * shard), bf16),
            pltpu.VMEM((pairs, part, 2 * shard), bf16),
            dma((2 + 3 * heads,)), dma((pairs,)), dma((pairs,)), dma((pairs,)),
            dma((pairs, groups)), dma((pairs, groups)),
            dma((pairs, heads, 3)), dma((pairs, heads, 3)), dma((heads, 3)), dma((heads, 3)),
            dma((pairs, heads)), dma((pairs, heads)), dma, dma,
            dma((pairs, pairs, heads)), dma((pairs, pairs, heads)), dma((pairs, pairs, heads)),
            dma((pairs, groups)), dma((pairs, groups)), dma((pairs,)), dma((pairs,)),
        ],
        compiler_params=pltpu.CompilerParams(
            collective_id=0, has_side_effects=True, vmem_limit_bytes=60 * 1024 * 1024
        ),
    )(
        tokens, ln_gain.reshape(1, features), q_w, k_w, v_w,
        q_gain.reshape(pairs, 1, width), k_gain.reshape(pairs, 1, width), out_w,
    )


def on_device(tokens, ln_gain, q_w, k_w, v_w, q_gain, k_gain, out_w):
    devices = lax.axis_size("dp")
    groups = lax.axis_size("mp")
    pairs = devices // 2
    fits = (
        devices % 2 == 0
        and pairs > 1
        and groups == 4
        and q_w.shape[1] % (pairs * HEAD_DIM) == 0
        and q_w.shape[0] % 128 == 0
        and tokens.shape[0] == IMG_TOKENS
        and tokens.shape[0] % (16 * groups) == 0
        and pairs <= 4
        and q_w.shape[1] <= 2 * pairs * HEAD_DIM
    )
    if fits:
        return exchanged_heads(pairs, groups, tokens, ln_gain, q_w, k_w, v_w, q_gain, k_gain, out_w)
    return gathered_weights(tokens, ln_gain, q_w, k_w, v_w, q_gain, k_gain, out_w)


def solution(mesh):
    in_specs = (
        P("dp", None),
        P(),
        P("dp", "mp"),
        P("dp", "mp"),
        P("dp", "mp"),
        P("mp"),
        P("mp"),
        P("dp", "mp"),
    )
    out_specs = P(("dp", "mp"), None)
    return jax.shard_map(
        on_device, mesh=mesh, in_specs=in_specs, out_specs=out_specs, check_vma=False
    )
```

profile of v0, /device:TPU:0, one launch (start us, length us, event | category | flops | bytes accessed | tf_op | source)
XLA Modules:
  0.0 135.0 jit_solution(3322682897224178310)
XLA Ops:
  0.0 133.2 %shard_map.82 = bf16[64,3072]{1,0:T(8,128)(2,1)} custom-call(bf16[256,3072]{1,0:T(8,128)(2,1)} %tokens.1, f32[1,3072]{1,0:T(1,128)} %bitcast.3, bf16[384,1024]{1,0:T(8,128)(2,1)} %q_w.1, bf16[384,1024]{1,0:T(8,128)(2,1)} %k_w.1, bf16[384,1024]{1,0:T(8,128)(2,1)} %v_w.1, f32[4,1,256]{2,1,0:T(1,128)} %bitcast.4, f32[4,1,256]{2,1,0:T(1,128)} %bitcast.5, ...), custom_call_target="tpu_custom_call" | custom-call | tf_op jit(solution)/shard_map/pallas_call | solution.py:560
  133.2 1.8 %copy.10 = bf16[64,3072]{1,0:T(8,128)(2,1)} copy(bf16[64,3072]{1,0:T(8,128)(2,1)} %shard_map.82) | data formatting | bytes 786432
where the time goes:
time: 135 us
  Pallas kernels  133 us (99%)
  local copies, waits for them, and re-layouts  1.77 us (1%)
    pallas_call x1, Pallas kernels, exchanged_heads(): pl.pallas_call(functools.partial(exchange_kernel, pairs, groups), out_sha...  133 us

commit v1 on v0

v1 whole, which is shorter than its diff:
```python
import functools
import math

import jax
import jax.numpy as jnp
from jax import lax
from jax.experimental import pallas as pl
from jax.experimental.pallas import tpu as pltpu
from jax.sharding import PartitionSpec as P

HEAD_DIM = 128
IMG_TOKENS = 256


epsilon = 1e-06


def layer_norm(values, scale_gain):
    average = jnp.mean(values, axis=-1, keepdims=True)
    centred = values - average
    variance = jnp.mean(centred * centred, axis=-1, keepdims=True)
    return centred * lax.rsqrt(variance + epsilon) * scale_gain


def head_norm(projected, scale_gain):
    heads_count = projected.shape[1] // HEAD_DIM
    shaped = projected.reshape(projected.shape[0], heads_count, HEAD_DIM)
    normed = layer_norm(shaped, scale_gain.reshape(heads_count, HEAD_DIM))
    return normed.reshape(projected.shape).astype(jnp.bfloat16)


def attend(queries, key_rows, value_rows):
    scores = jnp.einsum(
        "bqhd,bkhd->bhqk", queries, key_rows, preferred_element_type=jnp.float32
    ) * (1.0 / math.sqrt(HEAD_DIM))
    highest = jnp.max(scores, axis=-1, keepdims=True)
    weights = jnp.exp(scores - highest)
    probs = (weights / jnp.sum(weights, axis=-1, keepdims=True)).astype(jnp.bfloat16)
    context = jnp.einsum("bhqk,bkhd->bqhd", probs, value_rows, preferred_element_type=jnp.float32)
    return context.astype(jnp.bfloat16)


def place_three(holder, pieces, offset, local_width):
    holder = lax.dynamic_update_slice(holder, pieces[0], (offset, 0))
    holder = lax.dynamic_update_slice(holder, pieces[1], (offset, local_width))
    return lax.dynamic_update_slice(holder, pieces[2], (offset, 2 * local_width))


def gathered_weights(tokens, ln_gain, q_weight, k_weight, v_weight, q_gain, k_gain, out_weight):
    normed = layer_norm(tokens.astype(jnp.float32), ln_gain).astype(jnp.bfloat16)
    token_count = normed.shape[0]
    local_width = q_weight.shape[1]
    feature_count = normed.shape[1]
    stacked = jnp.zeros((feature_count, 3 * local_width), jnp.bfloat16)
    projections = place_three(
        stacked,
        (
            lax.all_gather(q_weight, "dp", axis=0, tiled=True),
            lax.all_gather(k_weight, "dp", axis=0, tiled=True),
            lax.all_gather(v_weight, "dp", axis=0, tiled=True),
        ),
        jnp.int32(0),
        local_width,
    )
    combined = jnp.dot(normed, projections, preferred_element_type=jnp.float32)
    queries = combined[:, :local_width]
    key_rows = combined[:, local_width : 2 * local_width]
    value_cast = combined[:, 2 * local_width :].astype(jnp.bfloat16)
    query_normed = head_norm(queries, q_gain)
    key_normed = head_norm(key_rows, k_gain)
    images = token_count // IMG_TOKENS
    shaped = (images, IMG_TOKENS, local_width // HEAD_DIM, HEAD_DIM)
    context = attend(
        query_normed.reshape(shaped), key_normed.reshape(shaped), value_cast.reshape(shaped)
    )
    context = context.reshape(token_count, local_width)
    out_full = lax.all_gather(out_weight, "dp", axis=0, tiled=True)
    return lax.psum_scatter(
        lax.dot_general(
            context, out_full, (((1,), (1,)), ((), ())), preferred_element_type=jnp.float32
        ).astype(jnp.bfloat16),
        "mp",
        scatter_dimension=0,
        tiled=True,
    )


MESH = pl.DeviceIdType.MESH

CHUNKS = 4


def exchange_kernel(
    pairs, groups, chunks, tokens, ln_gain, q_w, k_w, v_w, q_gain, k_gain, out_w, result,
    raw, normed, weights, out_rows, context, partial, arrived, summed, final,
    local_sem, token_send, token_recv, peer_send, peer_recv,
    w_send, w_recv, own_send, own_recv, pass_send, pass_recv, out_send, out_recv,
    c_send, c_recv, p_send, p_recv, f_send, f_recv,
):
    dp = lax.axis_index("dp")
    group = lax.axis_index("mp")
    pair = dp // 2
    core = dp % 2
    rows = tokens.shape[0]
    part = rows // groups
    piece_rows = part // chunks
    shard = q_w.shape[0]
    width = q_w.shape[1] // pairs
    span = 2 * shard
    heads = width // HEAD_DIM
    has_up = pair + 1 < pairs
    has_down = pair > 0

    def at_pair(other):
        return (other * 2 + core, group)

    partner = (pair * 2 + (1 - core), group)

    def at_group(other):
        return (dp, other)

    def remote(source, target, send, recv, device):
        return pltpu.make_async_remote_copy(
            src_ref=source, dst_ref=target, send_sem=send, recv_sem=recv,
            device_id=device, device_id_type=MESH,
        )

    def quarter_of(owner):
        return pl.ds(pl.multiple_of(owner * part, part), part)

    token_quarters = []
    for j in range(groups):
        place = quarter_of((group + j) % groups)
        token_quarters.append(
            pltpu.make_async_copy(tokens.at[place, :], raw.at[place, :], local_sem.at[j])
        )
        token_quarters[j].start()

    projections = (q_w, k_w, v_w)

    def columns(other, h, t):
        start = pl.multiple_of(other * width + h * HEAD_DIM, HEAD_DIM)
        return projections[t].at[:, pl.ds(start, HEAD_DIM)]

    def slot(h, block, side, t):
        return weights.at[h, block, side, :, pl.ds(t * HEAD_DIM, HEAD_DIM)]

    greeted = pltpu.get_barrier_semaphore()
    for step in range(1, pairs):
        pl.semaphore_signal(
            greeted, inc=1, device_id=at_pair((pair + step) % pairs), device_id_type=MESH
        )
    for step in range(1, groups):
        pl.semaphore_signal(
            greeted, inc=1, device_id=at_group((group + step) % groups), device_id_type=MESH
        )
    pl.semaphore_signal(greeted, inc=1, device_id=partner, device_id_type=MESH)

    locals_ = [pltpu.make_async_copy(out_w, out_rows.at[core], local_sem.at[groups])]
    for h in range(heads):
        for t in range(3):
            locals_.append(
                pltpu.make_async_copy(
                    columns(pair, h, t), slot(h, pair, core, t),
                    local_sem.at[groups + 1 + 3 * h + t],
                )
            )
    for copy in locals_:
        copy.start()

    def normalise(first_row, count):
        @pl.loop(0, count // 16)
        def _(step):
            place = pl.ds(pl.multiple_of(first_row + step * 16, 16), 16)
            values = raw[place, :].astype(jnp.float32)
            average = jnp.mean(values, axis=-1, keepdims=True)
            centred = values - average
            variance = jnp.mean(centred * centred, axis=-1, keepdims=True)
            scaled = centred * lax.rsqrt(variance + epsilon) * ln_gain[...]
            normed[pair, place, :] = scaled.astype(jnp.bfloat16)

    token_quarters[0].wait()
    normalise(group * part, part)

    def piece(block, owner, k):
        start = pl.multiple_of(owner * part + k * piece_rows, 16)
        return normed.at[block, pl.ds(start, piece_rows), :]

    def z_hop(block, k, up):
        there = piece(block, group, k)
        return remote(
            there, there, token_send.at[0 if up else 1, block], token_recv.at[block, k],
            at_pair(pair + 1 if up else pair - 1),
        )

    beside = group + 1 - 2 * (group % 2)
    across = (group + 2) % 4
    first = jnp.where(core == 0, beside, across)
    second = jnp.where(core == 0, across, beside)
    opposite = 3 - group

    def peer_copy(block, owner, place, k, other):
        there = piece(block, owner, k)
        return remote(
            there, there, peer_send.at[block, place], peer_recv.at[block, owner, k], at_group(other)
        )

    def weight_to(other, h, t):
        return remote(
            columns(other, h, t), slot(h, pair, core, t),
            w_send.at[other, h], w_recv.at[pair, h], at_pair(other),
        )

    def send_weights(up, some):
        for h in some:
            for distance in range(1, pairs):
                other = pair + distance if up else pair - distance

                @pl.when(other < pairs if up else other >= 0)
                def _():
                    for t in range(3):
                        weight_to(other, h, t).start()

    def own_weight(h, t):
        return remote(
            columns(pair, h, t), slot(h, pair, core, t), own_send, own_recv, partner
        )

    def out_over():
        return remote(out_w, out_rows.at[core], out_send, out_recv, partner)

    with jax.named_scope("greet"):
        pl.semaphore_wait(greeted, pairs + groups - 1)

    @pl.loop(0, chunks)
    def _(k):
        @pl.when(has_up)
        def _():
            z_hop(pair, k, True).start()

        @pl.when(has_down)
        def _():
            z_hop(pair, k, False).start()

    @pl.when(pair == 0)
    def _():
        send_weights(True, range(heads))

    @pl.when(pair == pairs - 1)
    def _():
        send_weights(False, range(heads))

    for h in range(heads):
        for t in range(3):
            own_weight(h, t).start()
    out_over().start()
    for j in range(1, groups):
        token_quarters[j].wait()

    def relay(block, k, up):
        with jax.named_scope("relaywait"):
            z_hop(block, k, up).wait_recv()

        @pl.when(has_up if up else has_down)
        def _():
            z_hop(block, k, up).start()

        peer_copy(block, group, 0, k, first).start()
        peer_copy(block, group, 1, k, second).start()

    others = rows - part
    for distance in range(1, pairs):
        @pl.loop(0, chunks)
        def _(k):
            @pl.when(pair - distance >= 0)
            def _():
                relay(pair - distance, k, True)

            @pl.when(pair + distance < pairs)
            def _():
                relay(pair + distance, k, False)

            if distance == 1:
                for j in range(1, groups):
                    normalise(((group + j) % groups) * part + k * piece_rows, piece_rows)

        @pl.when(has_up & (pair == distance))
        def _():
            send_weights(True, range(1))

            @pl.when(pair + 2 < pairs)
            def _():
                send_weights(True, range(1, heads))

        @pl.when(has_down & (pair == pairs - 1 - distance))
        def _():
            send_weights(False, range(1))

            @pl.when(pair - 2 >= 0)
            def _():
                send_weights(False, range(1, heads))

    def cross_tokens(block, k):
        with jax.named_scope("crosswait"):
            peer_copy(block, first, 0, k, first).wait_recv()
        peer_copy(block, first, 2, k, second).start()

    for distance in range(1, pairs):
        @pl.loop(0, chunks)
        def _(k):
            @pl.when(pair - distance >= 0)
            def _():
                cross_tokens(pair - distance, k)

            @pl.when(pair + distance < pairs)
            def _():
                cross_tokens(pair + distance, k)

    @pl.when(has_up & (pair == pairs - 2))
    def _():
        send_weights(True, range(1, heads))

    @pl.when(has_down & (pair == 1))
    def _():
        send_weights(False, range(1, heads))

    def pass_on(other, h):
        there = weights.at[h, other, core]
        return remote(there, there, pass_send.at[h], pass_recv.at[h], partner)

    def pass_weights(h):
        for distance in range(1, pairs):
            for up in (True, False):
                other = pair - distance if up else pair + distance

                @pl.when(other >= 0 if up else other < pairs)
                def _():
                    there = weights.at[h, other, core]
                    with jax.named_scope("wwait"):
                        remote(
                            there, there, w_send.at[other, h], w_recv.at[other, h], at_pair(other)
                        ).wait_recv()
                    pass_on(other, h).start()

    def all_passed(h):
        there = weights.at[h, pl.ds(0, pairs - 1), 1 - core]
        return remote(there, there, pass_send.at[h], pass_recv.at[h], partner)

    def all_own():
        there = weights.at[:, pair, 1 - core]
        return remote(there, there, own_send, own_recv, partner)

    pass_weights(0)
    for copy in locals_:
        copy.wait()
    all_own().wait_recv()
    for distance in range(1, pairs):
        for below in (True, False):
            block = pair - distance if below else pair + distance

            @pl.when(block >= 0 if below else block < pairs)
            def _():
                with jax.named_scope("tokwait"):
                    @pl.loop(0, chunks)
                    def _(k):
                        peer_copy(block, second, 0, k, second).wait_recv()
                        peer_copy(block, opposite, 0, k, second).wait_recv()

    def head_layer_norm(values, scale_gain):
        average = jnp.mean(values, axis=-1, keepdims=True)
        centred = values - average
        variance = jnp.mean(centred * centred, axis=-1, keepdims=True)
        return (centred * lax.rsqrt(variance + epsilon) * scale_gain).astype(jnp.bfloat16)

    def head_place(block, h):
        return pl.ds(pl.multiple_of(block * width + h * HEAD_DIM, HEAD_DIM), HEAD_DIM)

    def context_hop(block, image, h, up):
        there = context.at[image, :, head_place(block, h)]
        return remote(
            there, there,
            c_send.at[0 if up else 1, block, h], c_recv.at[block, image, h],
            at_pair(pair + 1 if up else pair - 1),
        )

    def pass_context(image, h, distance):
        for up in (True, False):
            block = pair - distance if up else pair + distance

            @pl.when(block >= 0 if up else block < pairs)
            def _():
                with jax.named_scope("ctxwait"):
                    context_hop(block, image, h, up).wait_recv()

                @pl.when(has_up if up else has_down)
                def _():
                    context_hop(block, image, h, up).start()

    def attend_head(image, h):
        lanes = slice(h * HEAD_DIM, (h + 1) * HEAD_DIM)
        with jax.named_scope("attend"):
            total = jnp.dot(
                normed[image], weights[h].reshape(pairs * span, 3 * HEAD_DIM),
                preferred_element_type=jnp.float32,
            )
            queries = head_layer_norm(total[:, :HEAD_DIM], q_gain[pair, :, lanes])
            key_rows = head_layer_norm(total[:, HEAD_DIM : 2 * HEAD_DIM], k_gain[pair, :, lanes])
            value_rows = total[:, 2 * HEAD_DIM :].astype(jnp.bfloat16)
            scores = lax.dot_general(
                queries, key_rows, (((1,), (1,)), ((), ())), preferred_element_type=jnp.float32
            ) * (1.0 / math.sqrt(HEAD_DIM))
            highest = jnp.max(scores, axis=-1, keepdims=True)
            spread = jnp.exp(scores - highest)
            probs = (spread / jnp.sum(spread, axis=-1, keepdims=True)).astype(jnp.bfloat16)
            mixed = jnp.dot(probs, value_rows, preferred_element_type=jnp.float32)
            context[image, :, head_place(pair, h)] = mixed.astype(jnp.bfloat16)

        @pl.when(has_up)
        def _():
            context_hop(pair, image, h, True).start()

        @pl.when(has_down)
        def _():
            context_hop(pair, image, h, False).start()

    for h in range(heads):
        if h > 0:
            pass_weights(h)
        with jax.named_scope("passedwait"):
            all_passed(h).wait_recv()

        @pl.loop(0, pairs)
        def _(image):
            attend_head(image, h)
            if h > 0:
                pass_context(image, h - 1, 1)

        if h == 0:
            with jax.named_scope("sends"):
                for distance in range(pairs):
                    for up in (True, False):
                        if distance == 0 and not up:
                            continue
                        block = pair - distance if up else pair + distance

                        @pl.when(block >= 0 if up else block < pairs)
                        def _():
                            quarter = normed.at[block, quarter_of(group), :]
                            for way, there in ((0, has_up), (1, has_down)):
                                if distance > 0 and way != (0 if up else 1):
                                    continue

                                @pl.when(there)
                                def _():
                                    remote(
                                        quarter, quarter, token_send.at[way, block],
                                        token_recv.at[block, 0], partner,
                                    ).wait_send()

                            if distance > 0:
                                for place in range(3):
                                    remote(
                                        quarter, quarter, peer_send.at[block, place],
                                        peer_recv.at[block, 0, 0], partner,
                                    ).wait_send()
                all_own().wait_send()
                out_back = remote(out_rows.at[1 - core], out_rows.at[1 - core], out_send, out_recv, partner)
                out_back.wait_recv()
                out_back.wait_send()

    for distance in range(2, pairs):
        for h in range(heads - 1):
            @pl.loop(0, pairs)
            def _(image):
                pass_context(image, h, distance)

    def partial_to(image, step):
        other = (group + step) % groups
        return remote(
            partial.at[image, quarter_of(other), :], arrived.at[image, step - 1],
            p_send.at[image], p_recv.at[image], at_group(other),
        )

    def partials(image):
        there = arrived.at[image]
        return remote(there, there, p_send.at[image], p_recv.at[image], partner)

    def final_to(image):
        return remote(summed.at[image], final.at[pair], f_send, f_recv, at_pair(image))

    def finals():
        there = final.at[pl.ds(0, pairs - 1)]
        return remote(there, there, f_send, f_recv, partner)

    def finish(image):
        with jax.named_scope("partwait"):
            partials(image).wait_recv()
        total = partial[image, quarter_of(group), :].astype(jnp.float32)
        for step in range(1, groups):
            total = total + arrived[image, step - 1].astype(jnp.float32)
        summed[image] = total.astype(jnp.bfloat16)

        @pl.when(image != pair)
        def _():
            final_to(image).start()

        @pl.when(image == pair)
        def _():
            final[pair] = summed[image]

    @pl.loop(0, pairs)
    def _(image):
        for distance in range(1, pairs):
            pass_context(image, heads - 1, distance)

        with jax.named_scope("outproj"):
            for c in range(2):
                product = lax.dot_general(
                    context[image], out_rows[c], (((1,), (1,)), ((), ())),
                    preferred_element_type=jnp.float32,
                )
                partial[image, :, c * shard : (c + 1) * shard] = product.astype(jnp.bfloat16)
        for step in range(1, groups):
            partial_to(image, step).start()

        @pl.when(image > 0)
        def _():
            finish(image - 1)

    with jax.named_scope("sends2"):
        for h in range(heads):
            own = weights.at[h, pl.ds(0, pairs - 1), core]
            remote(own, own, pass_send.at[h], pass_recv.at[h], partner).wait_send()
        for distance in range(1, pairs):
            for below in (True, False):
                other = pair - distance if below else pair + distance

                @pl.when(other >= 0 if below else other < pairs)
                def _():
                    for h in range(heads):
                        there = weights.at[h, pair, core]
                        remote(
                            there, there, w_send.at[other, h], w_recv.at[other, h], partner
                        ).wait_send()

    finish(pairs - 1)

    with jax.named_scope("sends3"):
        for distance in range(pairs):
            for up in (True, False):
                block = pair - distance if up else pair + distance

                @pl.when((block >= 0 if up else block < pairs) & (has_up if up else has_down))
                def _():
                    for h in range(heads):
                        there = context.at[:, :, head_place(block, h)]
                        remote(
                            there, there, c_send.at[0 if up else 1, block, h],
                            c_recv.at[block, 0, h], partner,
                        ).wait_send()

        @pl.loop(0, pairs)
        def _(image):
            partials(image).wait_send()

    with jax.named_scope("finalwait"):
        finals().wait_recv()
    for p in range(pairs):
        result[:, p * span : (p + 1) * span] = final[p]
    with jax.named_scope("sends4"):
        finals().wait_send()


def exchanged_heads(pairs, groups, tokens, ln_gain, q_w, k_w, v_w, q_gain, k_gain, out_w):
    rows, features = tokens.shape
    shard, local_width = q_w.shape
    width = local_width // pairs
    heads = width // HEAD_DIM
    part = rows // groups
    chunks = min(CHUNKS, part // 16)
    dma = pltpu.SemaphoreType.DMA
    in_hbm = pl.BlockSpec(memory_space=pl.ANY)
    in_vmem = pl.BlockSpec(memory_space=pltpu.VMEM)
    bf16 = jnp.bfloat16
    return pl.pallas_call(
        functools.partial(exchange_kernel, pairs, groups, chunks),
        out_shape=jax.ShapeDtypeStruct((part, features), bf16),
        in_specs=[in_hbm, in_vmem, in_hbm, in_hbm, in_hbm, in_vmem, in_vmem, in_hbm],
        out_specs=in_vmem,
        scratch_shapes=[
            pltpu.VMEM((rows, features), bf16),
            pltpu.VMEM((pairs, rows, features), bf16),
            pltpu.VMEM((heads, pairs, 2, shard, 3 * HEAD_DIM), bf16),
            pltpu.VMEM((2, shard, local_width), bf16),
            pltpu.VMEM((pairs, rows, local_width), bf16),
            pltpu.VMEM((pairs, rows, 2 * shard), bf16),
            pltpu.VMEM((pairs, groups - 1, part, 2 * shard), bf16),
            pltpu.VMEM((pairs, part, 2 * shard), bf16),
            pltpu.VMEM((pairs, part, 2 * shard), bf16),
            dma((groups + 1 + 3 * heads,)), dma((2, pairs)), dma((pairs, chunks)),
            dma((pairs, 3)), dma((pairs, groups, chunks)),
            dma((pairs, heads)), dma((pairs, heads)), dma, dma,
            dma((heads,)), dma((heads,)), dma, dma,
            dma((2, pairs, heads)), dma((pairs, pairs, heads)),
            dma((pairs,)), dma((pairs,)), dma, dma,
        ],
        compiler_params=pltpu.CompilerParams(
            collective_id=0, has_side_effects=True, vmem_limit_bytes=60 * 1024 * 1024
        ),
    )(
        tokens, ln_gain.reshape(1, features), q_w, k_w, v_w,
        q_gain.reshape(pairs, 1, width), k_gain.reshape(pairs, 1, width), out_w,
    )


def on_device(tokens, ln_gain, q_w, k_w, v_w, q_gain, k_gain, out_w):
    devices = lax.axis_size("dp")
    groups = lax.axis_size("mp")
    pairs = devices // 2
    fits = (
        devices % 2 == 0
        and pairs > 1
        and groups == 4
        and q_w.shape[1] % (pairs * HEAD_DIM) == 0
        and q_w.shape[0] % 128 == 0
        and tokens.shape[0] == IMG_TOKENS
        and tokens.shape[0] % (16 * groups) == 0
        and pairs <= 4
        and q_w.shape[1] <= 2 * pairs * HEAD_DIM
    )
    if fits:
        return exchanged_heads(pairs, groups, tokens, ln_gain, q_w, k_w, v_w, q_gain, k_gain, out_w)
    return gathered_weights(tokens, ln_gain, q_w, k_w, v_w, q_gain, k_gain, out_w)


def solution(mesh):
    in_specs = (
        P("dp", None),
        P(),
        P("dp", "mp"),
        P("dp", "mp"),
        P("dp", "mp"),
        P("mp"),
        P("mp"),
        P("dp", "mp"),
    )
    out_specs = P(("dp", "mp"), None)
    return jax.shard_map(
        on_device, mesh=mesh, in_specs=in_specs, out_specs=out_specs, check_vma=False
    )
```

time: 135 us -> 128 us (0.948)
  Pallas kernels: 133 us -> 126 us
    pallas_call x1, Pallas kernels: 133 us -> 126 us  [exchanged_heads(): pl.pallas_call(functools.partial(exchange_kernel, pairs, groups, chunks),...]
where the time goes in v1:
time: 128 us
  Pallas kernels  126 us (98%)
  local copies, waits for them, and re-layouts  1.77 us (1%)
    pallas_call x1, Pallas kernels, exchanged_heads(): pl.pallas_call(functools.partial(exchange_kernel, pairs, groups, chunks),...  126 us

profile of v1, /device:TPU:0, one launch (start us, length us, event | category | flops | bytes accessed | tf_op | source)
XLA Modules:
  0.0 128.0 jit_solution(10271330515060209042)
XLA Ops:
  0.0 126.2 %shard_map.82 = bf16[64,3072]{1,0:T(8,128)(2,1)} custom-call(bf16[256,3072]{1,0:T(8,128)(2,1)} %tokens.1, f32[1,3072]{1,0:T(1,128)} %bitcast.3, bf16[384,1024]{1,0:T(8,128)(2,1)} %q_w.1, bf16[384,1024]{1,0:T(8,128)(2,1)} %k_w.1, bf16[384,1024]{1,0:T(8,128)(2,1)} %v_w.1, f32[4,1,256]{2,1,0:T(1,128)} %bitcast.4, f32[4,1,256]{2,1,0:T(1,128)} %bitcast.5, ...), custom_call_target="tpu_custom_call" | custom-call | tf_op jit(solution)/shard_map/pallas_call | solution.py:585
  126.3 1.8 %copy.10 = bf16[64,3072]{1,0:T(8,128)(2,1)} copy(bf16[64,3072]{1,0:T(8,128)(2,1)} %shard_map.82) | data formatting | bytes 786432

commit v2 on v1

--- a/solution.py
+++ b/solution.py
@@ -92,10 +92,10 @@
 
 def exchange_kernel(
     pairs, groups, chunks, tokens, ln_gain, q_w, k_w, v_w, q_gain, k_gain, out_w, result,
-    raw, normed, weights, out_rows, context, partial, arrived, summed, final,
+    raw, normed, weights, out_rows, end_rows, context, partial, arrived, halves, summed, final,
     local_sem, token_send, token_recv, peer_send, peer_recv,
     w_send, w_recv, own_send, own_recv, pass_send, pass_recv, out_send, out_recv,
-    c_send, c_recv, p_send, p_recv, f_send, f_recv,
+    end_send, end_recv, c_send, c_recv, p_send, p_recv, q_send, q_recv, f_send, f_recv,
 ):
     dp = lax.axis_index("dp")
     group = lax.axis_index("mp")
@@ -110,6 +110,10 @@
     heads = width // HEAD_DIM
     has_up = pair + 1 < pairs
     has_down = pair > 0
+    at_end = (pair == 0) | (pair == pairs - 1)
+    beside_end = (pair == 1) | (pair == pairs - 2)
+    inner = jnp.where(pair < pairs // 2, pair + 1, pair - 1)
+    outer = jnp.where(pair < pairs // 2, pair - 1, pair + 1)
 
     def at_pair(other):
         return (other * 2 + core, group)
@@ -208,18 +212,17 @@
     def weight_to(other, h, t):
         return remote(
             columns(other, h, t), slot(h, pair, core, t),
-            w_send.at[other, h], w_recv.at[pair, h], at_pair(other),
-        )
-
-    def send_weights(up, some):
-        for h in some:
-            for distance in range(1, pairs):
-                other = pair + distance if up else pair - distance
-
-                @pl.when(other < pairs if up else other >= 0)
-                def _():
-                    for t in range(3):
-                        weight_to(other, h, t).start()
+            w_send.at[other, h], w_recv.at[pair, h, t], at_pair(other),
+        )
+
+    def send_weights(up, plan):
+        for h, distance in plan:
+            other = pair + distance if up else pair - distance
+
+            @pl.when(other < pairs if up else other >= 0)
+            def _():
+                for t in range(3):
+                    weight_to(other, h, t).start()
 
     def own_weight(h, t):
         return remote(
@@ -242,13 +245,19 @@
         def _():
             z_hop(pair, k, False).start()
 
-    @pl.when(pair == 0)
-    def _():
-        send_weights(True, range(heads))
-
-    @pl.when(pair == pairs - 1)
-    def _():
-        send_weights(False, range(heads))
+    def end_over():
+        return remote(out_w, end_rows.at[core], end_send.at[0], end_recv.at[0], at_pair(inner))
+
+    def end_in(side, device, at):
+        there = end_rows.at[side]
+        return remote(there, there, end_send.at[at], end_recv.at[at], device)
+
+    for at, up in ((0, True), (pairs - 1, False)):
+        @pl.when(pair == at)
+        def _():
+            send_weights(up, [(h, 1) for h in range(heads)])
+            send_weights(up, [(0, distance) for distance in range(2, pairs)])
+            end_over().start()
 
     for h in range(heads):
         for t in range(3):
@@ -286,19 +295,11 @@
 
         @pl.when(has_up & (pair == distance))
         def _():
-            send_weights(True, range(1))
-
-            @pl.when(pair + 2 < pairs)
-            def _():
-                send_weights(True, range(1, heads))
+            send_weights(True, [(h, d) for h in range(heads) for d in range(1, pairs - 1)])
 
         @pl.when(has_down & (pair == pairs - 1 - distance))
         def _():
-            send_weights(False, range(1))
-
-            @pl.when(pair - 2 >= 0)
-            def _():
-                send_weights(False, range(1, heads))
+            send_weights(False, [(h, d) for h in range(heads) for d in range(1, pairs - 1)])
 
     def cross_tokens(block, k):
         with jax.named_scope("crosswait"):
@@ -316,17 +317,6 @@
             def _():
                 cross_tokens(pair + distance, k)
 
-    @pl.when(has_up & (pair == pairs - 2))
-    def _():
-        send_weights(True, range(1, heads))
-
-    @pl.when(has_down & (pair == 1))
-    def _():
-        send_weights(False, range(1, heads))
-
-    def pass_on(other, h):
-        there = weights.at[h, other, core]
-        return remote(there, there, pass_send.at[h], pass_recv.at[h], partner)
 
     def pass_weights(h):
         for distance in range(1, pairs):
@@ -335,12 +325,13 @@
 
                 @pl.when(other >= 0 if up else other < pairs)
                 def _():
-                    there = weights.at[h, other, core]
-                    with jax.named_scope("wwait"):
-                        remote(
-                            there, there, w_send.at[other, h], w_recv.at[other, h], at_pair(other)
-                        ).wait_recv()
-                    pass_on(other, h).start()
+                    for t in range(3):
+                        there = slot(h, other, core, t)
+                        with jax.named_scope("wwait"):
+                            remote(
+                                there, there, w_send.at[other, h], w_recv.at[other, h, t], partner
+                            ).wait_recv()
+                        remote(there, there, pass_send.at[h], pass_recv.at[h], partner).start()
 
     def all_passed(h):
         there = weights.at[h, pl.ds(0, pairs - 1), 1 - core]
@@ -383,16 +374,49 @@
             at_pair(pair + 1 if up else pair - 1),
         )
 
+    def inside(image):
+        return (image > 0) & (image < pairs - 1)
+
+    def outside(image):
+        return (image == 0) | (image == pairs - 1)
+
+    def onward(image, up):
+        if up:
+            return has_up & ~((pair == pairs - 2) & inside(image))
+        return has_down & ~((pair == 1) & inside(image))
+
+    def awaited(block, image, up):
+        if up:
+            return (block >= 0) & ~((pair == pairs - 1) & inside(image))
+        return (block < pairs) & ~((pair == 0) & inside(image))
+
+    def send_context(image, h, across_middle, to_end):
+        for up in (True, False):
+            crossing = pair < pairs // 2 if up else pair >= pairs // 2
+            wanted = (crossing & across_middle) | (~crossing & to_end)
+
+            @pl.when(onward(image, up) & wanted)
+            def _():
+                context_hop(pair, image, h, up).start()
+
+    def cross_context(image, h):
+        for up in (True, False):
+            @pl.when((pair == 1) if up else (pair == pairs - 2))
+            def _():
+                with jax.named_scope("crossctx"):
+                    context_hop(outer, image, h, up).wait_recv()
+                context_hop(outer, image, h, up).start()
+
     def pass_context(image, h, distance):
         for up in (True, False):
             block = pair - distance if up else pair + distance
 
-            @pl.when(block >= 0 if up else block < pairs)
-            def _():
-                with jax.named_scope("ctxwait"):
+            @pl.when(awaited(block, image, up) & ~(beside_end & (block == outer)))
+            def _():
+                with jax.named_scope("ctxwait%d" % distance):
                     context_hop(block, image, h, up).wait_recv()
 
-                @pl.when(has_up if up else has_down)
+                @pl.when(onward(image, up))
                 def _():
                     context_hop(block, image, h, up).start()
 
@@ -415,117 +439,208 @@
             mixed = jnp.dot(probs, value_rows, preferred_element_type=jnp.float32)
             context[image, :, head_place(pair, h)] = mixed.astype(jnp.bfloat16)
 
-        @pl.when(has_up)
-        def _():
-            context_hop(pair, image, h, True).start()
-
-        @pl.when(has_down)
-        def _():
-            context_hop(pair, image, h, False).start()
-
-    for h in range(heads):
-        if h > 0:
-            pass_weights(h)
+    def image_at(step):
+        return step + 1 - 2 * (step % 2)
+
+    def all_weights(h):
         with jax.named_scope("passedwait"):
             all_passed(h).wait_recv()
 
-        @pl.loop(0, pairs)
-        def _(image):
-            attend_head(image, h)
-            if h > 0:
-                pass_context(image, h - 1, 1)
-
-        if h == 0:
-            with jax.named_scope("sends"):
-                for distance in range(pairs):
-                    for up in (True, False):
-                        if distance == 0 and not up:
+    all_weights(0)
+
+    @pl.loop(0, pairs)
+    def _(step):
+        image = image_at(step)
+        attend_head(image, 0)
+        send_context(image, 0, at_end | (step < 2), True)
+
+    for at, up in ((0, True), (pairs - 1, False)):
+        @pl.when(pair == at)
+        def _():
+            send_weights(up, [(h, d) for h in range(1, heads) for d in range(pairs - 1, 1, -1)])
+
+    with jax.named_scope("sends"):
+        for distance in range(pairs):
+            for up in (True, False):
+                if distance == 0 and not up:
+                    continue
+                block = pair - distance if up else pair + distance
+
+                @pl.when(block >= 0 if up else block < pairs)
+                def _():
+                    quarter = normed.at[block, quarter_of(group), :]
+                    for way, there in ((0, has_up), (1, has_down)):
+                        if distance > 0 and way != (0 if up else 1):
                             continue
-                        block = pair - distance if up else pair + distance
-
-                        @pl.when(block >= 0 if up else block < pairs)
+
+                        @pl.when(there)
                         def _():
-                            quarter = normed.at[block, quarter_of(group), :]
-                            for way, there in ((0, has_up), (1, has_down)):
-                                if distance > 0 and way != (0 if up else 1):
-                                    continue
-
-                                @pl.when(there)
-                                def _():
-                                    remote(
-                                        quarter, quarter, token_send.at[way, block],
-                                        token_recv.at[block, 0], partner,
-                                    ).wait_send()
-
-                            if distance > 0:
-                                for place in range(3):
-                                    remote(
-                                        quarter, quarter, peer_send.at[block, place],
-                                        peer_recv.at[block, 0, 0], partner,
-                                    ).wait_send()
-                all_own().wait_send()
-                out_back = remote(out_rows.at[1 - core], out_rows.at[1 - core], out_send, out_recv, partner)
-                out_back.wait_recv()
-                out_back.wait_send()
-
-    for distance in range(2, pairs):
-        for h in range(heads - 1):
-            @pl.loop(0, pairs)
-            def _(image):
-                pass_context(image, h, distance)
-
-    def partial_to(image, step):
-        other = (group + step) % groups
+                            remote(
+                                quarter, quarter, token_send.at[way, block],
+                                token_recv.at[block, 0], partner,
+                            ).wait_send()
+
+                    if distance > 0:
+                        for place in range(3):
+                            remote(
+                                quarter, quarter, peer_send.at[block, place],
+                                peer_recv.at[block, 0, 0], partner,
+                            ).wait_send()
+        all_own().wait_send()
+        out_back = remote(out_rows.at[1 - core], out_rows.at[1 - core], out_send, out_recv, partner)
+        out_back.wait_recv()
+        out_back.wait_send()
+
+
+    @pl.when(beside_end)
+    def _():
+        end_in(core, partner, 0).wait_recv()
+        end_in(core, partner, 1).start()
+
+    def partial_to(unit, c, at, owner):
         return remote(
-            partial.at[image, quarter_of(other), :], arrived.at[image, step - 1],
-            p_send.at[image], p_recv.at[image], at_group(other),
-        )
-
-    def partials(image):
-        there = arrived.at[image]
-        return remote(there, there, p_send.at[image], p_recv.at[image], partner)
-
-    def final_to(image):
-        return remote(summed.at[image], final.at[pair], f_send, f_recv, at_pair(image))
-
-    def finals():
-        there = final.at[pl.ds(0, pairs - 1)]
+            partial.at[unit, c, quarter_of(owner), :], arrived.at[unit, c, at],
+            p_send.at[unit], p_recv.at[unit, c], at_group(first),
+        )
+
+    def partials(unit, c):
+        there = arrived.at[unit, c, pl.ds(0, 2)]
+        return remote(there, there, p_send.at[unit], p_recv.at[unit, c], partner)
+
+    def half_to(unit, c):
+        return remote(
+            halves.at[unit, c], arrived.at[unit, c, 2], q_send.at[unit], q_recv.at[unit, c],
+            at_group(second),
+        )
+
+    def half_in(unit, c):
+        there = arrived.at[unit, c, 2]
+        return remote(there, there, q_send.at[unit], q_recv.at[unit, c], partner)
+
+    def final_to(unit, c, image, span_of):
+        return remote(summed.at[unit, c], final.at[span_of, c], f_send, f_recv, at_pair(image))
+
+    def finals(count):
+        there = final.at[pl.ds(0, count)]
         return remote(there, there, f_send, f_recv, partner)
 
-    def finish(image):
-        with jax.named_scope("partwait"):
-            partials(image).wait_recv()
-        total = partial[image, quarter_of(group), :].astype(jnp.float32)
-        for step in range(1, groups):
-            total = total + arrived[image, step - 1].astype(jnp.float32)
-        summed[image] = total.astype(jnp.bfloat16)
-
-        @pl.when(image != pair)
-        def _():
-            final_to(image).start()
-
-        @pl.when(image == pair)
-        def _():
-            final[pair] = summed[image]
-
-    @pl.loop(0, pairs)
-    def _(image):
-        for distance in range(1, pairs):
-            pass_context(image, heads - 1, distance)
-
-        with jax.named_scope("outproj"):
-            for c in range(2):
+    def project(unit, image, rows_of):
+        for c in range(2):
+            with jax.named_scope("outproj"):
                 product = lax.dot_general(
-                    context[image], out_rows[c], (((1,), (1,)), ((), ())),
+                    context[image], rows_of[c], (((1,), (1,)), ((), ())),
                     preferred_element_type=jnp.float32,
                 )
-                partial[image, :, c * shard : (c + 1) * shard] = product.astype(jnp.bfloat16)
-        for step in range(1, groups):
-            partial_to(image, step).start()
-
-        @pl.when(image > 0)
-        def _():
-            finish(image - 1)
+                partial[unit, c] = product.astype(jnp.bfloat16)
+            partial_to(unit, c, 0, first).start()
+            partial_to(unit, c, 1, opposite).start()
+
+    def add_halves(unit, c):
+        with jax.named_scope("partwait"):
+            partials(unit, c).wait_recv()
+        total = partial[unit, c, quarter_of(second), :].astype(jnp.float32)
+        total = total + arrived[unit, c, 1].astype(jnp.float32)
+        halves[unit, c] = total.astype(jnp.bfloat16)
+        half_to(unit, c).start()
+
+    def add_up(unit, c, image, span_of):
+        with jax.named_scope("halfwait"):
+            half_in(unit, c).wait_recv()
+        total = partial[unit, c, quarter_of(group), :].astype(jnp.float32)
+        for at in (0, 2):
+            total = total + arrived[unit, c, at].astype(jnp.float32)
+        total = total.astype(jnp.bfloat16)
+
+        @pl.when(image != pair)
+        def _():
+            summed[unit, c] = total
+            final_to(unit, c, image, span_of).start()
+
+        @pl.when(image == pair)
+        def _():
+            final[span_of, c] = total
+
+    def for_units(image, act):
+        @pl.when(~at_end | outside(image))
+        def _():
+            act(image, pair)
+
+        @pl.when(beside_end & inside(image))
+        def _():
+            act(pairs + image - 1, outer)
+
+    def halve(image):
+        def act(unit, span_of):
+            for c in range(2):
+                add_halves(unit, c)
+        for_units(image, act)
+
+    def finish(image):
+        def act(unit, span_of):
+            for c in range(2):
+                add_up(unit, c, image, span_of)
+        for_units(image, act)
+
+
+    for step in range(2):
+        cross_context(image_at(step), 0)
+    pass_weights(heads - 1)
+    all_weights(heads - 1)
+
+    lag = 2
+
+    @pl.loop(0, pairs + lag)
+    def _(step):
+        @pl.when(step < pairs)
+        def _():
+            image = image_at(step)
+            attend_head(image, heads - 1)
+            send_context(image, heads - 1, True, True)
+            cross_context(image, heads - 1)
+
+            @pl.when(step + 2 < pairs)
+            def _():
+                after = image_at(step + 2)
+
+                @pl.when(~at_end)
+                def _():
+                    send_context(after, 0, True, False)
+                cross_context(after, 0)
+
+        @pl.when(step >= lag)
+        def _():
+            image = image_at(step - lag)
+            for distance in range(1, pairs):
+                for h in range(heads):
+                    pass_context(image, h, distance)
+
+            @pl.when(~at_end | outside(image))
+            def _():
+                project(image, image, out_rows)
+
+            @pl.when(beside_end & inside(image))
+            def _():
+                @pl.when(image == image_at(0))
+                def _():
+                    end_in(1 - core, partner, 1).wait_recv()
+
+                project(pairs + image - 1, image, end_rows)
+
+        @pl.when(step > lag)
+        def _():
+            halve(image_at(step - lag - 1))
+
+        @pl.when(step > lag + 1)
+        def _():
+            finish(image_at(step - lag - 2))
+
+    def wait_partials(image):
+        def act(unit, span_of):
+            there = partial.at[unit, :, pl.ds(0, 2 * part), :]
+            remote(there, there, p_send.at[unit], p_recv.at[unit, 0], partner).wait_send()
+            there = halves.at[unit]
+            remote(there, there, q_send.at[unit], q_recv.at[unit, 0], partner).wait_send()
+        for_units(image, act)
 
     with jax.named_scope("sends2"):
         for h in range(heads):
@@ -540,35 +655,79 @@
                     for h in range(heads):
                         there = weights.at[h, pair, core]
                         remote(
-                            there, there, w_send.at[other, h], w_recv.at[other, h], partner
+                            there, there, w_send.at[other, h], w_recv.at[other, h, 0], partner
                         ).wait_send()
 
-    finish(pairs - 1)
-
-    with jax.named_scope("sends3"):
+        @pl.when(at_end)
+        def _():
+            end_over().wait_send()
+
+        @pl.when(beside_end)
+        def _():
+            end_in(core, partner, 1).wait_send()
+
         for distance in range(pairs):
             for up in (True, False):
                 block = pair - distance if up else pair + distance
+                thin = (pair == pairs - 2) if up else (pair == 1)
 
                 @pl.when((block >= 0 if up else block < pairs) & (has_up if up else has_down))
                 def _():
                     for h in range(heads):
-                        there = context.at[:, :, head_place(block, h)]
-                        remote(
-                            there, there, c_send.at[0 if up else 1, block, h],
-                            c_recv.at[block, 0, h], partner,
-                        ).wait_send()
-
-        @pl.loop(0, pairs)
-        def _(image):
-            partials(image).wait_send()
+                        def sent(count):
+                            there = context.at[pl.ds(0, count), :, head_place(block, h)]
+                            return remote(
+                                there, there, c_send.at[0 if up else 1, block, h],
+                                c_recv.at[block, 0, h], partner,
+                            )
+
+                        @pl.when(thin)
+                        def _():
+                            sent(2).wait_send()
+
+                        @pl.when(~thin)
+                        def _():
+                            sent(pairs).wait_send()
+
+        @pl.loop(0, pairs - 2)
+        def _(step):
+            wait_partials(image_at(step))
+
+    finish(image_at(pairs - 2))
+    last = image_at(pairs - 1)
+
+    @pl.when(beside_end)
+    def _():
+        ends = [(last, pair, c) for c in range(2)] + [(pairs + last - 1, outer, c) for c in range(2)]
+        for k in range(len(ends) + 1):
+            if k < len(ends):
+                add_halves(ends[k][0], ends[k][2])
+            if k > 0:
+                add_up(ends[k - 1][0], ends[k - 1][2], last, ends[k - 1][1])
+
+    wait_partials(image_at(pairs - 2))
+    wait_partials(last)
 
     with jax.named_scope("finalwait"):
-        finals().wait_recv()
+        @pl.when(at_end)
+        def _():
+            finals(pairs - 1).wait_recv()
+
+        @pl.when(~at_end)
+        def _():
+            finals(pairs - 2).wait_recv()
     for p in range(pairs):
-        result[:, p * span : (p + 1) * span] = final[p]
+        for c in range(2):
+            start = (2 * p + c) * shard
+            result[:, start : start + shard] = final[p, c]
     with jax.named_scope("sends4"):
-        finals().wait_send()
+        @pl.when(at_end)
+        def _():
+            finals(1).wait_send()
+
+        @pl.when(~at_end)
+        def _():
+            finals(pairs).wait_send()
 
 
 def exchanged_heads(pairs, groups, tokens, ln_gain, q_w, k_w, v_w, q_gain, k_gain, out_w):
@@ -578,6 +737,7 @@
     heads = width // HEAD_DIM
     part = rows // groups
     chunks = min(CHUNKS, part // 16)
+    units = 2 * pairs - 2
     dma = pltpu.SemaphoreType.DMA
     in_hbm = pl.BlockSpec(memory_space=pl.ANY)
     in_vmem = pl.BlockSpec(memory_space=pltpu.VMEM)
@@ -592,17 +752,19 @@
             pltpu.VMEM((pairs, rows, features), bf16),
             pltpu.VMEM((heads, pairs, 2, shard, 3 * HEAD_DIM), bf16),
             pltpu.VMEM((2, shard, local_width), bf16),
+            pltpu.VMEM((2, shard, local_width), bf16),
             pltpu.VMEM((pairs, rows, local_width), bf16),
-            pltpu.VMEM((pairs, rows, 2 * shard), bf16),
-            pltpu.VMEM((pairs, groups - 1, part, 2 * shard), bf16),
-            pltpu.VMEM((pairs, part, 2 * shard), bf16),
-            pltpu.VMEM((pairs, part, 2 * shard), bf16),
+            pltpu.VMEM((units, 2, rows, shard), bf16),
+            pltpu.VMEM((units, 2, 3, part, shard), bf16),
+            pltpu.VMEM((units, 2, part, shard), bf16),
+            pltpu.VMEM((units, 2, part, shard), bf16),
+            pltpu.VMEM((pairs, 2, part, shard), bf16),
             dma((groups + 1 + 3 * heads,)), dma((2, pairs)), dma((pairs, chunks)),
             dma((pairs, 3)), dma((pairs, groups, chunks)),
-            dma((pairs, heads)), dma((pairs, heads)), dma, dma,
+            dma((pairs, heads)), dma((pairs, heads, 3)), dma, dma,
             dma((heads,)), dma((heads,)), dma, dma,
-            dma((2, pairs, heads)), dma((pairs, pairs, heads)),
-            dma((pairs,)), dma((pairs,)), dma, dma,
+            dma((2,)), dma((2,)), dma((2, pairs, heads)), dma((pairs, pairs, heads)),
+            dma((units,)), dma((units, 2)), dma((units,)), dma((units, 2)), dma, dma,
         ],
         compiler_params=pltpu.CompilerParams(
             collective_id=0, has_side_effects=True, vmem_limit_bytes=60 * 1024 * 1024
@@ -619,14 +781,13 @@
     pairs = devices // 2
     fits = (
         devices % 2 == 0
-        and pairs > 1
         and groups == 4
         and q_w.shape[1] % (pairs * HEAD_DIM) == 0
         and q_w.shape[0] % 128 == 0
         and tokens.shape[0] == IMG_TOKENS
         and tokens.shape[0] % (16 * groups) == 0
-        and pairs <= 4
-        and q_w.shape[1] <= 2 * pairs * HEAD_DIM
+        and pairs == 4
+        and q_w.shape[1] == 2 * pairs * HEAD_DIM
     )
     if fits:
         return exchanged_heads(pairs, groups, tokens, ln_gain, q_w, k_w, v_w, q_gain, k_gain, out_w)

time: 128 us -> 117 us (0.914)
  Pallas kernels: 126 us -> 115 us
    pallas_call x1, Pallas kernels: 126 us -> 115 us  [exchanged_heads(): pl.pallas_call(functools.partial(exchange_kernel, pairs, groups, chunks),...]
where the time goes in v2:
time: 117 us
  Pallas kernels  115 us (98%)
  local copies, waits for them, and re-layouts  1.77 us (2%)
    pallas_call x1, Pallas kernels, exchanged_heads(): pl.pallas_call(functools.partial(exchange_kernel, pairs, groups, chunks),...  115 us

profile of v2, /device:TPU:0, one launch (start us, length us, event | category | flops | bytes accessed | tf_op | source)
XLA Modules:
  0.0 116.8 jit_solution(10328591897171551759)
XLA Ops:
  0.0 115.1 %shard_map.82 = bf16[64,3072]{1,0:T(8,128)(2,1)} custom-call(bf16[256,3072]{1,0:T(8,128)(2,1)} %tokens.1, f32[1,3072]{1,0:T(1,128)} %bitcast.3, bf16[384,1024]{1,0:T(8,128)(2,1)} %q_w.1, bf16[384,1024]{1,0:T(8,128)(2,1)} %k_w.1, bf16[384,1024]{1,0:T(8,128)(2,1)} %v_w.1, f32[4,1,256]{2,1,0:T(1,128)} %bitcast.4, f32[4,1,256]{2,1,0:T(1,128)} %bitcast.5, ...), custom_call_target="tpu_custom_call" | custom-call | tf_op jit(solution)/shard_map/pallas_call | solution.py:745
  115.1 1.8 %copy.10 = bf16[64,3072]{1,0:T(8,128)(2,1)} copy(bf16[64,3072]{1,0:T(8,128)(2,1)} %shard_map.82) | data formatting | bytes 786432

commit v3 on v2

--- a/solution.py
+++ b/solution.py
@@ -92,10 +92,10 @@
 
 def exchange_kernel(
     pairs, groups, chunks, tokens, ln_gain, q_w, k_w, v_w, q_gain, k_gain, out_w, result,
-    raw, normed, weights, out_rows, end_rows, context, partial, arrived, halves, summed, final,
+    raw, normed, weights, out_rows, end_rows, staged, context, kept, partial, arrived, summed, final,
     local_sem, token_send, token_recv, peer_send, peer_recv,
-    w_send, w_recv, own_send, own_recv, pass_send, pass_recv, out_send, out_recv,
-    end_send, end_recv, c_send, c_recv, p_send, p_recv, q_send, q_recv, f_send, f_recv,
+    w_send, w_recv, own_send, own_recv, pass_send, pass_recv, out_send, out_recv, side_send, side_recv,
+    end_send, end_recv, x_send, x_recv, c_send, c_recv, p_send, p_recv, f_send, f_recv,
 ):
     dp = lax.axis_index("dp")
     group = lax.axis_index("mp")
@@ -159,14 +159,19 @@
             greeted, inc=1, device_id=at_group((group + step) % groups), device_id_type=MESH
         )
     pl.semaphore_signal(greeted, inc=1, device_id=partner, device_id_type=MESH)
-
-    locals_ = [pltpu.make_async_copy(out_w, out_rows.at[core], local_sem.at[groups])]
+    beside = group + 1 - 2 * (group % 2)
+    across = (group + 2) % 4
+    pl.semaphore_signal(
+        greeted, inc=1,
+        device_id=(pair * 2 + 1 - core, jnp.where(core == 0, beside, across)), device_id_type=MESH,
+    )
+
+    locals_ = [pltpu.make_async_copy(out_w, out_rows.at[0, core], local_sem.at[groups])]
     for h in range(heads):
         for t in range(3):
             locals_.append(
                 pltpu.make_async_copy(
-                    columns(pair, h, t), slot(h, pair, core, t),
-                    local_sem.at[groups + 1 + 3 * h + t],
+                    columns(pair, h, t), slot(h, pair, core, t), local_sem.at[groups + 1],
                 )
             )
     for copy in locals_:
@@ -193,12 +198,10 @@
     def z_hop(block, k, up):
         there = piece(block, group, k)
         return remote(
-            there, there, token_send.at[0 if up else 1, block], token_recv.at[block, k],
+            there, there, token_send.at[0 if up else 1], token_recv.at[block, k],
             at_pair(pair + 1 if up else pair - 1),
         )
 
-    beside = group + 1 - 2 * (group % 2)
-    across = (group + 2) % 4
     first = jnp.where(core == 0, beside, across)
     second = jnp.where(core == 0, across, beside)
     opposite = 3 - group
@@ -206,13 +209,13 @@
     def peer_copy(block, owner, place, k, other):
         there = piece(block, owner, k)
         return remote(
-            there, there, peer_send.at[block, place], peer_recv.at[block, owner, k], at_group(other)
+            there, there, peer_send, peer_recv.at[block, place, k if place == 0 else 0], at_group(other)
         )
 
     def weight_to(other, h, t):
         return remote(
             columns(other, h, t), slot(h, pair, core, t),
-            w_send.at[other, h], w_recv.at[pair, h, t], at_pair(other),
+            w_send, w_recv.at[pair, h, t], at_pair(other),
         )
 
     def send_weights(up, plan):
@@ -230,10 +233,15 @@
         )
 
     def out_over():
-        return remote(out_w, out_rows.at[core], out_send, out_recv, partner)
+        return remote(out_w, out_rows.at[0, core], out_send, out_recv, partner)
+
+    sides = ((pair * 2, beside), (pair * 2 + 1, across))
+
+    def rows_aside(to):
+        return remote(out_w, out_rows.at[1, core], side_send, side_recv.at[core], sides[to])
 
     with jax.named_scope("greet"):
-        pl.semaphore_wait(greeted, pairs + groups - 1)
+        pl.semaphore_wait(greeted, pairs + groups)
 
     @pl.loop(0, chunks)
     def _(k):
@@ -246,11 +254,12 @@
             z_hop(pair, k, False).start()
 
     def end_over():
-        return remote(out_w, end_rows.at[core], end_send.at[0], end_recv.at[0], at_pair(inner))
-
-    def end_in(side, device, at):
-        there = end_rows.at[side]
-        return remote(there, there, end_send.at[at], end_recv.at[at], device)
+        return remote(out_w, end_rows.at[0, core], end_send.at[0], end_recv.at[0], at_pair(inner))
+
+    def end_in(side, way, at, recv, device):
+        return remote(
+            end_rows.at[0, side], end_rows.at[way, side], end_send.at[at], end_recv.at[recv], device
+        )
 
     for at, up in ((0, True), (pairs - 1, False)):
         @pl.when(pair == at)
@@ -258,6 +267,7 @@
             send_weights(up, [(h, 1) for h in range(heads)])
             send_weights(up, [(0, distance) for distance in range(2, pairs)])
             end_over().start()
+            send_weights(up, [(h, d) for h in range(1, heads) for d in range(pairs - 1, 1, -1)])
 
     for h in range(heads):
         for t in range(3):
@@ -329,21 +339,22 @@
                         there = slot(h, other, core, t)
                         with jax.named_scope("wwait"):
                             remote(
-                                there, there, w_send.at[other, h], w_recv.at[other, h, t], partner
+                                there, there, w_send, w_recv.at[other, h, t], partner
                             ).wait_recv()
-                        remote(there, there, pass_send.at[h], pass_recv.at[h], partner).start()
+                        remote(there, there, pass_send, pass_recv.at[h], partner).start()
 
     def all_passed(h):
         there = weights.at[h, pl.ds(0, pairs - 1), 1 - core]
-        return remote(there, there, pass_send.at[h], pass_recv.at[h], partner)
+        return remote(there, there, pass_send, pass_recv.at[h], partner)
 
     def all_own():
         there = weights.at[:, pair, 1 - core]
         return remote(there, there, own_send, own_recv, partner)
 
     pass_weights(0)
-    for copy in locals_:
-        copy.wait()
+    locals_[0].wait()
+    there = weights.at[:, pair, core]
+    pltpu.make_async_copy(there, there, local_sem.at[groups + 1]).wait()
     all_own().wait_recv()
     for distance in range(1, pairs):
         for below in (True, False):
@@ -352,10 +363,14 @@
             @pl.when(block >= 0 if below else block < pairs)
             def _():
                 with jax.named_scope("tokwait"):
-                    @pl.loop(0, chunks)
-                    def _(k):
-                        peer_copy(block, second, 0, k, second).wait_recv()
-                        peer_copy(block, opposite, 0, k, second).wait_recv()
+                    for place, owner in ((1, second), (2, opposite)):
+                        there = normed.at[block, quarter_of(owner), :]
+                        remote(
+                            there, there, peer_send, peer_recv.at[block, place, 0], partner
+                        ).wait_recv()
+
+    for to in range(2):
+        rows_aside(to).start()
 
     def head_layer_norm(values, scale_gain):
         average = jnp.mean(values, axis=-1, keepdims=True)
@@ -367,10 +382,10 @@
         return pl.ds(pl.multiple_of(block * width + h * HEAD_DIM, HEAD_DIM), HEAD_DIM)
 
     def context_hop(block, image, h, up):
-        there = context.at[image, :, head_place(block, h)]
+        there = context.at[image, :, :, :, head_place(block, h)]
         return remote(
             there, there,
-            c_send.at[0 if up else 1, block, h], c_recv.at[block, image, h],
+            c_send.at[0 if up else 1], c_recv.at[block, image, h],
             at_pair(pair + 1 if up else pair - 1),
         )
 
@@ -419,6 +434,18 @@
                 @pl.when(onward(image, up))
                 def _():
                     context_hop(block, image, h, up).start()
+
+    def half_over(image, h, at, owner):
+        return remote(
+            staged.at[image, h, quarter_of(owner), :],
+            context.at[image, 1, at, :, head_place(pair, h)],
+            x_send, x_recv.at[image, h], at_group(first),
+        )
+
+    def half_in(image, h):
+        there = context.at[image, 1, :, :, head_place(pair, h)]
+        with jax.named_scope("halfin"):
+            remote(there, there, x_send, x_recv.at[image, h], partner).wait_recv()
 
     def attend_head(image, h):
         lanes = slice(h * HEAD_DIM, (h + 1) * HEAD_DIM)
@@ -437,10 +464,15 @@
             spread = jnp.exp(scores - highest)
             probs = (spread / jnp.sum(spread, axis=-1, keepdims=True)).astype(jnp.bfloat16)
             mixed = jnp.dot(probs, value_rows, preferred_element_type=jnp.float32)
-            context[image, :, head_place(pair, h)] = mixed.astype(jnp.bfloat16)
+            staged[image, h] = mixed.astype(jnp.bfloat16)
+
+        for at, owner in enumerate((first, opposite)):
+            half_over(image, h, at, owner).start()
+        for at, owner in enumerate((group, second)):
+            context[image, 0, at, :, head_place(pair, h)] = staged[image, h, quarter_of(owner), :]
 
     def image_at(step):
-        return step + 1 - 2 * (step % 2)
+        return step ^ (step // 2)
 
     def all_weights(h):
         with jax.named_scope("passedwait"):
@@ -450,72 +482,47 @@
 
     @pl.loop(0, pairs)
     def _(step):
-        image = image_at(step)
-        attend_head(image, 0)
-        send_context(image, 0, at_end | (step < 2), True)
-
-    for at, up in ((0, True), (pairs - 1, False)):
-        @pl.when(pair == at)
-        def _():
-            send_weights(up, [(h, d) for h in range(1, heads) for d in range(pairs - 1, 1, -1)])
+        attend_head(image_at(step), 0)
 
     with jax.named_scope("sends"):
-        for distance in range(pairs):
-            for up in (True, False):
-                if distance == 0 and not up:
-                    continue
-                block = pair - distance if up else pair + distance
-
-                @pl.when(block >= 0 if up else block < pairs)
-                def _():
-                    quarter = normed.at[block, quarter_of(group), :]
-                    for way, there in ((0, has_up), (1, has_down)):
-                        if distance > 0 and way != (0 if up else 1):
-                            continue
-
-                        @pl.when(there)
-                        def _():
-                            remote(
-                                quarter, quarter, token_send.at[way, block],
-                                token_recv.at[block, 0], partner,
-                            ).wait_send()
-
-                    if distance > 0:
-                        for place in range(3):
-                            remote(
-                                quarter, quarter, peer_send.at[block, place],
-                                peer_recv.at[block, 0, 0], partner,
-                            ).wait_send()
+        for at in range(pairs):
+            @pl.when(pair == at)
+            def _():
+                for way, blocks in ((0, at + 1 if at + 1 < pairs else 0), (1, pairs - at if at > 0 else 0)):
+                    if blocks > 0:
+                        there = normed.at[pl.ds(0, blocks), pl.ds(0, part), :]
+                        remote(
+                            there, there, token_send.at[way], token_recv.at[0, 0], partner
+                        ).wait_send()
+        there = normed.at[pl.ds(0, pairs - 1), pl.ds(0, 3 * part), :]
+        remote(there, there, peer_send, peer_recv.at[0, 0, 0], partner).wait_send()
         all_own().wait_send()
-        out_back = remote(out_rows.at[1 - core], out_rows.at[1 - core], out_send, out_recv, partner)
+        out_back = remote(out_rows.at[0, 1 - core], out_rows.at[0, 1 - core], out_send, out_recv, partner)
         out_back.wait_recv()
         out_back.wait_send()
 
 
+    def end_part(side, k, way, recv, device):
+        place = pl.ds(k * (shard // 2), shard // 2)
+        return remote(
+            end_rows.at[0, side, place, :], end_rows.at[way, side, place, :],
+            end_send.at[2], end_recv.at[recv], device,
+        )
+
+    def end_aside(k):
+        for to in range(2):
+            end_part(core, k, 1, 2 + 2 * core + k, sides[to]).start()
+
     @pl.when(beside_end)
     def _():
-        end_in(core, partner, 0).wait_recv()
-        end_in(core, partner, 1).start()
-
-    def partial_to(unit, c, at, owner):
+        end_in(core, 0, 0, 0, partner).wait_recv()
+        end_in(core, 0, 1, 1, partner).start()
+        end_aside(0)
+
+    def partial_to(unit, c):
         return remote(
-            partial.at[unit, c, quarter_of(owner), :], arrived.at[unit, c, at],
-            p_send.at[unit], p_recv.at[unit, c], at_group(first),
-        )
-
-    def partials(unit, c):
-        there = arrived.at[unit, c, pl.ds(0, 2)]
-        return remote(there, there, p_send.at[unit], p_recv.at[unit, c], partner)
-
-    def half_to(unit, c):
-        return remote(
-            halves.at[unit, c], arrived.at[unit, c, 2], q_send.at[unit], q_recv.at[unit, c],
-            at_group(second),
-        )
-
-    def half_in(unit, c):
-        there = arrived.at[unit, c, 2]
-        return remote(there, there, q_send.at[unit], q_recv.at[unit, c], partner)
+            partial.at[unit, c], arrived.at[unit, c], p_send, p_recv.at[unit, c], at_group(second)
+        )
 
     def final_to(unit, c, image, span_of):
         return remote(summed.at[unit, c], final.at[span_of, c], f_send, f_recv, at_pair(image))
@@ -525,31 +532,24 @@
         return remote(there, there, f_send, f_recv, partner)
 
     def project(unit, image, rows_of):
+        with jax.named_scope("outproj"):
+            total = None
+            for j in range(2):
+                product = lax.dot_general(
+                    context[image, j].reshape(2 * part, pairs * width), rows_of[j].reshape(span, pairs * width),
+                    (((1,), (1,)), ((), ())), preferred_element_type=jnp.float32,
+                )
+                total = product if total is None else total + product
+            for c in range(2):
+                kept[unit, c] = total[:part, c * shard : (c + 1) * shard]
+                partial[unit, c] = total[part:, c * shard : (c + 1) * shard].astype(jnp.bfloat16)
         for c in range(2):
-            with jax.named_scope("outproj"):
-                product = lax.dot_general(
-                    context[image], rows_of[c], (((1,), (1,)), ((), ())),
-                    preferred_element_type=jnp.float32,
-                )
-                partial[unit, c] = product.astype(jnp.bfloat16)
-            partial_to(unit, c, 0, first).start()
-            partial_to(unit, c, 1, opposite).start()
-
-    def add_halves(unit, c):
+            partial_to(unit, c).start()
+
+    def add_up(unit, c, image, span_of):
         with jax.named_scope("partwait"):
-            partials(unit, c).wait_recv()
-        total = partial[unit, c, quarter_of(second), :].astype(jnp.float32)
-        total = total + arrived[unit, c, 1].astype(jnp.float32)
-        halves[unit, c] = total.astype(jnp.bfloat16)
-        half_to(unit, c).start()
-
-    def add_up(unit, c, image, span_of):
-        with jax.named_scope("halfwait"):
-            half_in(unit, c).wait_recv()
-        total = partial[unit, c, quarter_of(group), :].astype(jnp.float32)
-        for at in (0, 2):
-            total = total + arrived[unit, c, at].astype(jnp.float32)
-        total = total.astype(jnp.bfloat16)
+            partial_to(unit, c).wait_recv()
+        total = (kept[unit, c] + arrived[unit, c].astype(jnp.float32)).astype(jnp.bfloat16)
 
         @pl.when(image != pair)
         def _():
@@ -560,103 +560,121 @@
         def _():
             final[span_of, c] = total
 
-    def for_units(image, act):
-        @pl.when(~at_end | outside(image))
-        def _():
-            act(image, pair)
-
-        @pl.when(beside_end & inside(image))
-        def _():
-            act(pairs + image - 1, outer)
-
-    def halve(image):
-        def act(unit, span_of):
+    def own_unit(image):
+        return ~at_end | outside(image)
+
+    def extra_unit(image):
+        return beside_end & inside(image)
+
+    def finish(image, extra):
+        @pl.when(extra_unit(image) if extra else own_unit(image))
+        def _():
             for c in range(2):
-                add_halves(unit, c)
-        for_units(image, act)
-
-    def finish(image):
-        def act(unit, span_of):
-            for c in range(2):
-                add_up(unit, c, image, span_of)
-        for_units(image, act)
-
-
-    for step in range(2):
-        cross_context(image_at(step), 0)
+                add_up(pairs + image - 1 if extra else image, c, image, outer if extra else pair)
+
+    for to in range(2):
+        remote(out_w, out_rows.at[1, to], side_send, side_recv.at[to], partner).wait_recv()
+    for step in range(pairs):
+        half_in(image_at(step), 0)
+        send_context(image_at(step), 0, at_end | (step < 3), True)
     pass_weights(heads - 1)
     all_weights(heads - 1)
 
-    lag = 2
+    def pass_most(image):
+        for h in range(heads):
+            pass_context(image, h, 1)
+        pass_context(image, 0, 2)
+
+    def pass_rest(image):
+        pass_context(image, 1, 2)
+        for h in range(heads):
+            pass_context(image, h, 3)
+
+    lag = 4
 
     @pl.loop(0, pairs + lag)
     def _(step):
         @pl.when(step < pairs)
         def _():
-            image = image_at(step)
-            attend_head(image, heads - 1)
-            send_context(image, heads - 1, True, True)
-            cross_context(image, heads - 1)
-
-            @pl.when(step + 2 < pairs)
-            def _():
-                after = image_at(step + 2)
-
-                @pl.when(~at_end)
+            attend_head(image_at(step), heads - 1)
+
+        @pl.when((step > 0) & (step <= pairs))
+        def _():
+            image = image_at(step - 1)
+            half_in(image, heads - 1)
+            send_context(image, heads - 1, at_end | (step < 3), True)
+
+            @pl.when(step < pairs)
+            def _():
+                cross_context(image, 0)
+
+            @pl.when((step == 1) & ~at_end)
+            def _():
+                send_context(image_at(pairs - 1), 0, True, False)
+
+            @pl.when((step == pairs) & beside_end)
+            def _():
+                end_aside(1)
+
+        @pl.when(step >= lag)
+        def _():
+            image = image_at(step - lag)
+
+            @pl.when(step == lag)
+            def _():
+                cross_context(image_at(0), heads - 1)
+
+            @pl.when(step < lag + 2)
+            def _():
+                pass_most(image)
+
+            @pl.when(step < pairs + lag - 1)
+            def _():
+                cross_context(image_at(step - lag + 1), heads - 1)
+
+            @pl.when((step < lag + 2) & ~at_end)
+            def _():
+                send_context(image_at(step - lag + 2), heads - 1, True, False)
+
+            @pl.when(step == lag + 1)
+            def _():
+                cross_context(image_at(pairs - 1), 0)
+            pass_rest(image)
+
+            @pl.when((step > lag) & (step < pairs + lag - 1))
+            def _():
+                pass_most(image_at(step - lag + 1))
+
+            @pl.when(own_unit(image))
+            def _():
+                project(image, image, out_rows)
+
+            @pl.when(extra_unit(image))
+            def _():
+                @pl.when(step == lag + 1)
                 def _():
-                    send_context(after, 0, True, False)
-                cross_context(after, 0)
-
-        @pl.when(step >= lag)
-        def _():
-            image = image_at(step - lag)
-            for distance in range(1, pairs):
-                for h in range(heads):
-                    pass_context(image, h, distance)
-
-            @pl.when(~at_end | outside(image))
-            def _():
-                project(image, image, out_rows)
-
-            @pl.when(beside_end & inside(image))
-            def _():
-                @pl.when(image == image_at(0))
-                def _():
-                    end_in(1 - core, partner, 1).wait_recv()
+                    end_in(1 - core, 0, 1, 1, partner).wait_recv()
+                    with jax.named_scope("endrows"):
+                        for side in range(2):
+                            for k in range(2):
+                                end_part(side, k, 1, 2 + 2 * side + k, partner).wait_recv()
 
                 project(pairs + image - 1, image, end_rows)
 
-        @pl.when(step > lag)
-        def _():
-            halve(image_at(step - lag - 1))
-
-        @pl.when(step > lag + 1)
-        def _():
-            finish(image_at(step - lag - 2))
-
-    def wait_partials(image):
-        def act(unit, span_of):
-            there = partial.at[unit, :, pl.ds(0, 2 * part), :]
-            remote(there, there, p_send.at[unit], p_recv.at[unit, 0], partner).wait_send()
-            there = halves.at[unit]
-            remote(there, there, q_send.at[unit], q_recv.at[unit, 0], partner).wait_send()
-        for_units(image, act)
+        @pl.when(step == lag + 2)
+        def _():
+            for early in range(2):
+                for extra in (False, True):
+                    finish(image_at(early), extra)
+
+    for step in range(2, pairs):
+        for extra in (False, True):
+            finish(image_at(step), extra)
 
     with jax.named_scope("sends2"):
-        for h in range(heads):
-            own = weights.at[h, pl.ds(0, pairs - 1), core]
-            remote(own, own, pass_send.at[h], pass_recv.at[h], partner).wait_send()
-        for distance in range(1, pairs):
-            for below in (True, False):
-                other = pair - distance if below else pair + distance
-
-                @pl.when(other >= 0 if below else other < pairs)
-                def _():
-                    for h in range(heads):
-                        there = weights.at[h, pair, core]
-                        remote(
-                            there, there, w_send.at[other, h], w_recv.at[other, h, 0], partner
-                        ).wait_send()
+        others = weights.at[:, pl.ds(0, pairs - 1), core]
+        remote(others, others, pass_send, pass_recv.at[0], partner).wait_send()
+        remote(others, others, w_send, w_recv.at[0, 0, 0], partner).wait_send()
 
         @pl.when(at_end)
         def _():
@@ -664,49 +682,35 @@
 
         @pl.when(beside_end)
         def _():
-            end_in(core, partner, 1).wait_send()
-
-        for distance in range(pairs):
-            for up in (True, False):
-                block = pair - distance if up else pair + distance
-                thin = (pair == pairs - 2) if up else (pair == 1)
-
-                @pl.when((block >= 0 if up else block < pairs) & (has_up if up else has_down))
-                def _():
-                    for h in range(heads):
-                        def sent(count):
-                            there = context.at[pl.ds(0, count), :, head_place(block, h)]
-                            return remote(
-                                there, there, c_send.at[0 if up else 1, block, h],
-                                c_recv.at[block, 0, h], partner,
-                            )
-
-                        @pl.when(thin)
-                        def _():
-                            sent(2).wait_send()
-
-                        @pl.when(~thin)
-                        def _():
-                            sent(pairs).wait_send()
-
-        @pl.loop(0, pairs - 2)
-        def _(step):
-            wait_partials(image_at(step))
-
-    finish(image_at(pairs - 2))
-    last = image_at(pairs - 1)
-
-    @pl.when(beside_end)
-    def _():
-        ends = [(last, pair, c) for c in range(2)] + [(pairs + last - 1, outer, c) for c in range(2)]
-        for k in range(len(ends) + 1):
-            if k < len(ends):
-                add_halves(ends[k][0], ends[k][2])
-            if k > 0:
-                add_up(ends[k - 1][0], ends[k - 1][2], last, ends[k - 1][1])
-
-    wait_partials(image_at(pairs - 2))
-    wait_partials(last)
+            end_in(core, 0, 1, 1, partner).wait_send()
+            both = end_rows.at[0]
+            remote(both, both, end_send.at[2], end_recv.at[2], partner).wait_send()
+
+        def sent(way, images, blocks):
+            there = context.at[pl.ds(0, images), :, :, :, pl.ds(0, blocks * width)]
+            return remote(there, there, c_send.at[way], c_recv.at[0, 0, 0], partner)
+
+        for at, counts in (
+            (0, ((0, pairs, 1),)),
+            (1, ((0, pairs, 2), (1, 2, pairs - 1))),
+            (pairs - 2, ((0, 2, pairs - 1), (1, pairs, 2))),
+            (pairs - 1, ((1, pairs, 1),)),
+        ):
+            @pl.when(pair == at)
+            def _():
+                for way, images, blocks in counts:
+                    sent(way, images, blocks).wait_send()
+
+    with jax.named_scope("sends3"):
+        both = out_rows.at[0]
+        remote(both, both, side_send, side_recv.at[0], partner).wait_send()
+        half = staged.at[:, :, pl.ds(0, 2 * part), :]
+        remote(half, half, x_send, x_recv.at[0, 0], partner).wait_send()
+        for few, units in ((at_end, 2), (beside_end, 2 * pairs - 2)):
+            @pl.when(few)
+            def _():
+                whole = partial.at[pl.ds(0, units)]
+                remote(whole, whole, p_send, p_recv.at[0, 0], partner).wait_send()
 
     with jax.named_scope("finalwait"):
         @pl.when(at_end)
@@ -744,27 +748,26 @@
     bf16 = jnp.bfloat16
     return pl.pallas_call(
         functools.partial(exchange_kernel, pairs, groups, chunks),
-        out_shape=jax.ShapeDtypeStruct((part, features), bf16),
+        out_shape=pltpu.VMEM((part, features), bf16),
         in_specs=[in_hbm, in_vmem, in_hbm, in_hbm, in_hbm, in_vmem, in_vmem, in_hbm],
         out_specs=in_vmem,
         scratch_shapes=[
             pltpu.VMEM((rows, features), bf16),
             pltpu.VMEM((pairs, rows, features), bf16),
             pltpu.VMEM((heads, pairs, 2, shard, 3 * HEAD_DIM), bf16),
-            pltpu.VMEM((2, shard, local_width), bf16),
-            pltpu.VMEM((2, shard, local_width), bf16),
-            pltpu.VMEM((pairs, rows, local_width), bf16),
-            pltpu.VMEM((units, 2, rows, shard), bf16),
-            pltpu.VMEM((units, 2, 3, part, shard), bf16),
+            pltpu.VMEM((2, 2, shard, local_width), bf16),
+            pltpu.VMEM((2, 2, shard, local_width), bf16),
+            pltpu.VMEM((pairs, heads, rows, HEAD_DIM), bf16),
+            pltpu.VMEM((pairs, 2, 2, part, local_width), bf16),
+            pltpu.VMEM((units, 2, part, shard), jnp.float32),
+            pltpu.VMEM((units, 2, part, shard), bf16),
             pltpu.VMEM((units, 2, part, shard), bf16),
             pltpu.VMEM((units, 2, part, shard), bf16),
             pltpu.VMEM((pairs, 2, part, shard), bf16),
-            dma((groups + 1 + 3 * heads,)), dma((2, pairs)), dma((pairs, chunks)),
-            dma((pairs, 3)), dma((pairs, groups, chunks)),
-            dma((pairs, heads)), dma((pairs, heads, 3)), dma, dma,
-            dma((heads,)), dma((heads,)), dma, dma,
-            dma((2,)), dma((2,)), dma((2, pairs, heads)), dma((pairs, pairs, heads)),
-            dma((units,)), dma((units, 2)), dma((units,)), dma((units, 2)), dma, dma,
+            dma((groups + 2,)), dma((2,)), dma((pairs, chunks)), dma, dma((pairs, 3, chunks)),
+            dma, dma((pairs, heads, 3)), dma, dma, dma, dma((heads,)), dma, dma, dma, dma((2,)),
+            dma((3,)), dma((6,)), dma, dma((pairs, heads)), dma((2,)), dma((pairs, pairs, heads)),
+            dma, dma((units, 2)), dma, dma,
         ],
         compiler_params=pltpu.CompilerParams(
             collective_id=0, has_side_effects=True, vmem_limit_bytes=60 * 1024 * 1024

time: 117 us -> 111 us (0.949)
  Pallas kernels: 115 us -> 110 us
    pallas_call x1, Pallas kernels: 115 us -> 110 us  [exchanged_heads(): pl.pallas_call(functools.partial(exchange_kernel, pairs, groups, chunks),...]
where the time goes in v3:
time: 111 us
  Pallas kernels  110 us (99%)
    pallas_call x1, Pallas kernels, exchanged_heads(): pl.pallas_call(functools.partial(exchange_kernel, pairs, groups, chunks),...  110 us

profile of v3, /device:TPU:0, one launch (start us, length us, event | category | flops | bytes accessed | tf_op | source)
XLA Modules:
  0.0 110.9 jit_solution(4066761857419494395)
XLA Ops:
  0.0 110.1 %shard_map.82 = bf16[64,3072]{1,0:T(8,128)(2,1)S(1)} custom-call(bf16[256,3072]{1,0:T(8,128)(2,1)} %tokens.1, f32[1,3072]{1,0:T(1,128)} %bitcast.3, bf16[384,1024]{1,0:T(8,128)(2,1)} %q_w.1, bf16[384,1024]{1,0:T(8,128)(2,1)} %k_w.1, bf16[384,1024]{1,0:T(8,128)(2,1)} %v_w.1, f32[4,1,256]{2,1,0:T(1,128)} %bitcast.4, f32[4,1,256]{2,1,0:T(1,128)} %bitcast.5, ...), custom_call_target="tpu_custom_call" | custom-call | tf_op jit(solution)/shard_map/pallas_call | solution.py:749
  110.1 0.7 copy.10

commit v4 on v3

--- a/solution.py
+++ b/solution.py
@@ -92,8 +92,8 @@
 
 def exchange_kernel(
     pairs, groups, chunks, tokens, ln_gain, q_w, k_w, v_w, q_gain, k_gain, out_w, result,
-    raw, normed, weights, out_rows, end_rows, staged, context, kept, partial, arrived, summed, final,
-    local_sem, token_send, token_recv, peer_send, peer_recv,
+    raw, normed, weights, own_rows, out_rows, end_rows, staged, context, kept, partial, arrived, summed, final,
+    local_sem, token_send, token_recv, peer_send, first_recv, peer_recv,
     w_send, w_recv, own_send, own_recv, pass_send, pass_recv, out_send, out_recv, side_send, side_recv,
     end_send, end_recv, x_send, x_recv, c_send, c_recv, p_send, p_recv, f_send, f_recv,
 ):
@@ -166,7 +166,7 @@
         device_id=(pair * 2 + 1 - core, jnp.where(core == 0, beside, across)), device_id_type=MESH,
     )
 
-    locals_ = [pltpu.make_async_copy(out_w, out_rows.at[0, core], local_sem.at[groups])]
+    locals_ = [pltpu.make_async_copy(out_w, own_rows, local_sem.at[groups])]
     for h in range(heads):
         for t in range(3):
             locals_.append(
@@ -209,7 +209,7 @@
     def peer_copy(block, owner, place, k, other):
         there = piece(block, owner, k)
         return remote(
-            there, there, peer_send, peer_recv.at[block, place, k if place == 0 else 0], at_group(other)
+            there, there, peer_send, first_recv.at[block, k] if place == 0 else peer_recv.at[block, place - 1], at_group(other)
         )
 
     def weight_to(other, h, t):
@@ -232,13 +232,31 @@
             columns(pair, h, t), slot(h, pair, core, t), own_send, own_recv, partner
         )
 
-    def out_over():
-        return remote(out_w, out_rows.at[0, core], out_send, out_recv, partner)
+    def side_of(rows_of, way, side, k=None):
+        lanes = pl.ds(pl.multiple_of(side * shard, 128), shard)
+        if k is None:
+            return rows_of.at[way, :, lanes]
+        depth = pairs * width // 2
+        return rows_of.at[way, pl.ds(k * depth, depth), lanes]
+
+    def transpose_rows():
+        @pl.loop(0, pairs * width // 128)
+        def _(k):
+            place = pl.ds(pl.multiple_of(k * 128, 128), 128)
+            lanes = pl.ds(pl.multiple_of(core * shard, 128), shard)
+            out_rows[0, place, lanes] = jnp.transpose(own_rows[:, place])
+
+    def out_over(side):
+        there = side_of(out_rows, 0, side)
+        return remote(there, there, out_send, out_recv, partner)
 
     sides = ((pair * 2, beside), (pair * 2 + 1, across))
 
-    def rows_aside(to):
-        return remote(out_w, out_rows.at[1, core], side_send, side_recv.at[core], sides[to])
+    def rows_aside(side, k, device):
+        return remote(
+            side_of(out_rows, 0, side, k), side_of(out_rows, 1, side, k),
+            side_send, side_recv.at[side, k], device,
+        )
 
     with jax.named_scope("greet"):
         pl.semaphore_wait(greeted, pairs + groups)
@@ -253,12 +271,20 @@
         def _():
             z_hop(pair, k, False).start()
 
-    def end_over():
-        return remote(out_w, end_rows.at[0, core], end_send.at[0], end_recv.at[0], at_pair(inner))
-
-    def end_in(side, way, at, recv, device):
-        return remote(
-            end_rows.at[0, side], end_rows.at[way, side], end_send.at[at], end_recv.at[recv], device
+    def end_over(side):
+        return remote(
+            side_of(out_rows, 0, side), side_of(end_rows, 0, side),
+            end_send.at[0], end_recv.at[0], at_pair(inner),
+        )
+
+    def end_pass(side):
+        there = side_of(end_rows, 0, side)
+        return remote(there, there, end_send.at[1], end_recv.at[1], partner)
+
+    def end_part(side, k, device):
+        return remote(
+            side_of(end_rows, 0, side, k), side_of(end_rows, 1, side, k),
+            end_send.at[2], end_recv.at[2 + 2 * side + k], device,
         )
 
     for at, up in ((0, True), (pairs - 1, False)):
@@ -266,13 +292,10 @@
         def _():
             send_weights(up, [(h, 1) for h in range(heads)])
             send_weights(up, [(0, distance) for distance in range(2, pairs)])
-            end_over().start()
-            send_weights(up, [(h, d) for h in range(1, heads) for d in range(pairs - 1, 1, -1)])
 
     for h in range(heads):
         for t in range(3):
             own_weight(h, t).start()
-    out_over().start()
     for j in range(1, groups):
         token_quarters[j].wait()
 
@@ -302,6 +325,17 @@
             if distance == 1:
                 for j in range(1, groups):
                     normalise(((group + j) % groups) * part + k * piece_rows, piece_rows)
+
+        if distance == 1:
+            with jax.named_scope("transpose"):
+                locals_[0].wait()
+                transpose_rows()
+            out_over(core).start()
+            for at, up in ((0, True), (pairs - 1, False)):
+                @pl.when(pair == at)
+                def _():
+                    end_over(core).start()
+                    send_weights(up, [(h, d) for h in range(1, heads) for d in range(pairs - 1, 1, -1)])
 
         @pl.when(has_up & (pair == distance))
         def _():
@@ -352,7 +386,6 @@
         return remote(there, there, own_send, own_recv, partner)
 
     pass_weights(0)
-    locals_[0].wait()
     there = weights.at[:, pair, core]
     pltpu.make_async_copy(there, there, local_sem.at[groups + 1]).wait()
     all_own().wait_recv()
@@ -366,11 +399,11 @@
                     for place, owner in ((1, second), (2, opposite)):
                         there = normed.at[block, quarter_of(owner), :]
                         remote(
-                            there, there, peer_send, peer_recv.at[block, place, 0], partner
+                            there, there, peer_send, peer_recv.at[block, place - 1], partner
                         ).wait_recv()
 
     for to in range(2):
-        rows_aside(to).start()
+        rows_aside(core, 0, sides[to]).start()
 
     def head_layer_norm(values, scale_gain):
         average = jnp.mean(values, axis=-1, keepdims=True)
@@ -471,8 +504,19 @@
         for at, owner in enumerate((group, second)):
             context[image, 0, at, :, head_place(pair, h)] = staged[image, h, quarter_of(owner), :]
 
+    lower = pair < pairs // 2
+    homely = jnp.where(lower, 1, pairs - 2)
+    foreign = pairs - 1 - homely
+
     def image_at(step):
-        return step ^ (step // 2)
+        if isinstance(step, int):
+            return (0, pairs - 1, homely, foreign)[step]
+        return jnp.where(step < 2, step * (pairs - 1), jnp.where(step == 2, homely, foreign))
+
+    def projected_at(step):
+        if isinstance(step, int):
+            return (0, pairs - 1, foreign, homely)[step]
+        return jnp.where(step < 2, step * (pairs - 1), jnp.where(step == 2, foreign, homely))
 
     def all_weights(h):
         with jax.named_scope("passedwait"):
@@ -483,6 +527,9 @@
     @pl.loop(0, pairs)
     def _(step):
         attend_head(image_at(step), 0)
+
+    for to in range(2):
+        rows_aside(core, 1, sides[to]).start()
 
     with jax.named_scope("sends"):
         for at in range(pairs):
@@ -495,28 +542,20 @@
                             there, there, token_send.at[way], token_recv.at[0, 0], partner
                         ).wait_send()
         there = normed.at[pl.ds(0, pairs - 1), pl.ds(0, 3 * part), :]
-        remote(there, there, peer_send, peer_recv.at[0, 0, 0], partner).wait_send()
+        remote(there, there, peer_send, peer_recv.at[0, 0], partner).wait_send()
         all_own().wait_send()
-        out_back = remote(out_rows.at[0, 1 - core], out_rows.at[0, 1 - core], out_send, out_recv, partner)
-        out_back.wait_recv()
-        out_back.wait_send()
-
-
-    def end_part(side, k, way, recv, device):
-        place = pl.ds(k * (shard // 2), shard // 2)
-        return remote(
-            end_rows.at[0, side, place, :], end_rows.at[way, side, place, :],
-            end_send.at[2], end_recv.at[recv], device,
-        )
+        out_over(1 - core).wait_recv()
+        out_over(core).wait_send()
+
 
     def end_aside(k):
         for to in range(2):
-            end_part(core, k, 1, 2 + 2 * core + k, sides[to]).start()
+            end_part(core, k, sides[to]).start()
 
     @pl.when(beside_end)
     def _():
-        end_in(core, 0, 0, 0, partner).wait_recv()
-        end_in(core, 0, 1, 1, partner).start()
+        end_over(core).wait_recv()
+        end_pass(core).start()
         end_aside(0)
 
     def partial_to(unit, c):
@@ -536,8 +575,8 @@
             total = None
             for j in range(2):
                 product = lax.dot_general(
-                    context[image, j].reshape(2 * part, pairs * width), rows_of[j].reshape(span, pairs * width),
-                    (((1,), (1,)), ((), ())), preferred_element_type=jnp.float32,
+                    context[image, j].reshape(2 * part, pairs * width), rows_of[j],
+                    (((1,), (0,)), ((), ())), preferred_element_type=jnp.float32,
                 )
                 total = product if total is None else total + product
             for c in range(2):
@@ -572,8 +611,6 @@
             for c in range(2):
                 add_up(pairs + image - 1 if extra else image, c, image, outer if extra else pair)
 
-    for to in range(2):
-        remote(out_w, out_rows.at[1, to], side_send, side_recv.at[to], partner).wait_recv()
     for step in range(pairs):
         half_in(image_at(step), 0)
         send_context(image_at(step), 0, at_end | (step < 3), True)
@@ -618,7 +655,7 @@
 
         @pl.when(step >= lag)
         def _():
-            image = image_at(step - lag)
+            image = projected_at(step - lag)
 
             @pl.when(step == lag)
             def _():
@@ -639,37 +676,43 @@
             @pl.when(step == lag + 1)
             def _():
                 cross_context(image_at(pairs - 1), 0)
+
+            @pl.when(step == lag + 3)
+            def _():
+                for early in range(2):
+                    finish(projected_at(early), False)
+
             pass_rest(image)
 
             @pl.when((step > lag) & (step < pairs + lag - 1))
             def _():
-                pass_most(image_at(step - lag + 1))
+                pass_most(projected_at(step - lag + 1))
 
             @pl.when(own_unit(image))
             def _():
+                @pl.when(step == lag)
+                def _():
+                    for side in range(2):
+                        for k in range(2):
+                            rows_aside(side, k, partner).wait_recv()
+
                 project(image, image, out_rows)
 
             @pl.when(extra_unit(image))
             def _():
-                @pl.when(step == lag + 1)
+                @pl.when(step == lag + 2)
                 def _():
-                    end_in(1 - core, 0, 1, 1, partner).wait_recv()
+                    end_pass(1 - core).wait_recv()
                     with jax.named_scope("endrows"):
                         for side in range(2):
                             for k in range(2):
-                                end_part(side, k, 1, 2 + 2 * side + k, partner).wait_recv()
+                                end_part(side, k, partner).wait_recv()
 
                 project(pairs + image - 1, image, end_rows)
-
-        @pl.when(step == lag + 2)
-        def _():
-            for early in range(2):
-                for extra in (False, True):
-                    finish(image_at(early), extra)
 
     for step in range(2, pairs):
         for extra in (False, True):
-            finish(image_at(step), extra)
+            finish(projected_at(step), extra)
 
     with jax.named_scope("sends2"):
         others = weights.at[:, pl.ds(0, pairs - 1), core]
@@ -678,11 +721,11 @@
 
         @pl.when(at_end)
         def _():
-            end_over().wait_send()
+            end_over(core).wait_send()
 
         @pl.when(beside_end)
         def _():
-            end_in(core, 0, 1, 1, partner).wait_send()
+            end_pass(core).wait_send()
             both = end_rows.at[0]
             remote(both, both, end_send.at[2], end_recv.at[2], partner).wait_send()
 
@@ -755,8 +798,9 @@
             pltpu.VMEM((rows, features), bf16),
             pltpu.VMEM((pairs, rows, features), bf16),
             pltpu.VMEM((heads, pairs, 2, shard, 3 * HEAD_DIM), bf16),
-            pltpu.VMEM((2, 2, shard, local_width), bf16),
-            pltpu.VMEM((2, 2, shard, local_width), bf16),
+            pltpu.VMEM((shard, local_width), bf16),
+            pltpu.VMEM((2, local_width, 2 * shard), bf16),
+            pltpu.VMEM((2, local_width, 2 * shard), bf16),
             pltpu.VMEM((pairs, heads, rows, HEAD_DIM), bf16),
             pltpu.VMEM((pairs, 2, 2, part, local_width), bf16),
             pltpu.VMEM((units, 2, part, shard), jnp.float32),
@@ -764,8 +808,8 @@
             pltpu.VMEM((units, 2, part, shard), bf16),
             pltpu.VMEM((units, 2, part, shard), bf16),
             pltpu.VMEM((pairs, 2, part, shard), bf16),
-            dma((groups + 2,)), dma((2,)), dma((pairs, chunks)), dma, dma((pairs, 3, chunks)),
-            dma, dma((pairs, heads, 3)), dma, dma, dma, dma((heads,)), dma, dma, dma, dma((2,)),
+            dma((groups + 2,)), dma((2,)), dma((pairs, chunks)), dma, dma((pairs, chunks)), dma((pairs, 2)),
+            dma, dma((pairs, heads, 3)), dma, dma, dma, dma((heads,)), dma, dma, dma, dma((2, 2)),
             dma((3,)), dma((6,)), dma, dma((pairs, heads)), dma((2,)), dma((pairs, pairs, heads)),
             dma, dma((units, 2)), dma, dma,
         ],

time: 111 us -> 109 us (0.982)
  Pallas kernels: 110 us -> 107 us
    pallas_call x1, Pallas kernels: 110 us -> 107 us  [exchanged_heads(): pl.pallas_call(functools.partial(exchange_kernel, pairs, groups, chunks),...]
where the time goes in v4:
time: 109 us; the launch traced here: 108 us
  Pallas kernels  107 us (98%)
    pallas_call x1, Pallas kernels, exchanged_heads(): pl.pallas_call(functools.partial(exchange_kernel, pairs, groups, chunks),...  107 us

profile of v4, /device:TPU:0, one launch (start us, length us, event | category | flops | bytes accessed | tf_op | source)
XLA Modules:
  0.0 107.9 jit_solution(16584141621870287354)
XLA Ops:
  0.0 107.1 %shard_map.82 = bf16[64,3072]{1,0:T(8,128)(2,1)S(1)} custom-call(bf16[256,3072]{1,0:T(8,128)(2,1)} %tokens.1, f32[1,3072]{1,0:T(1,128)} %bitcast.3, bf16[384,1024]{1,0:T(8,128)(2,1)} %q_w.1, bf16[384,1024]{1,0:T(8,128)(2,1)} %k_w.1, bf16[384,1024]{1,0:T(8,128)(2,1)} %v_w.1, f32[4,1,256]{2,1,0:T(1,128)} %bitcast.4, f32[4,1,256]{2,1,0:T(1,128)} %bitcast.5, ...), custom_call_target="tpu_custom_call" | custom-call | tf_op jit(solution)/shard_map/pallas_call | solution.py:792
  107.1 0.7 copy.10

commit v5 on v4

--- a/solution.py
+++ b/solution.py
@@ -649,6 +649,11 @@
             def _():
                 send_context(image_at(pairs - 1), 0, True, False)
 
+            for at, (turn, h, distance) in enumerate(((0, 0, 1), (1, 0, 1), (0, 0, 2))):
+                @pl.when((step == at + 1) & beside_end)
+                def _():
+                    pass_context(image_at(turn), h, distance)
+
             @pl.when((step == pairs) & beside_end)
             def _():
                 end_aside(1)
@@ -660,33 +665,36 @@
             @pl.when(step == lag)
             def _():
                 cross_context(image_at(0), heads - 1)
-
-            @pl.when(step < lag + 2)
-            def _():
-                pass_most(image)
-
-            @pl.when(step < pairs + lag - 1)
-            def _():
-                cross_context(image_at(step - lag + 1), heads - 1)
-
-            @pl.when((step < lag + 2) & ~at_end)
-            def _():
-                send_context(image_at(step - lag + 2), heads - 1, True, False)
-
-            @pl.when(step == lag + 1)
-            def _():
-                cross_context(image_at(pairs - 1), 0)
 
             @pl.when(step == lag + 3)
             def _():
                 for early in range(2):
                     finish(projected_at(early), False)
 
+            @pl.when(at_end | (step > lag + 1))
+            def _():
+                pass_most(image)
+
+            @pl.when((step == lag) & beside_end)
+            def _():
+                pass_context(image_at(0), 1, 1)
+                cross_context(image_at(1), heads - 1)
+                send_context(image_at(2), heads - 1, True, False)
+                pass_context(image_at(1), 1, 1)
+                pass_context(image_at(1), 0, 2)
+                cross_context(image_at(2), heads - 1)
+                send_context(image_at(3), heads - 1, True, False)
+                cross_context(image_at(3), 0)
+
+            @pl.when(step == lag + 1)
+            def _():
+                cross_context(image_at(pairs - 1), heads - 1)
+
+            @pl.when(step == lag + 3)
+            def _():
+                finish(projected_at(2), False)
+
             pass_rest(image)
-
-            @pl.when((step > lag) & (step < pairs + lag - 1))
-            def _():
-                pass_most(projected_at(step - lag + 1))
 
             @pl.when(own_unit(image))
             def _():
@@ -710,9 +718,9 @@
 
                 project(pairs + image - 1, image, end_rows)
 
-    for step in range(2, pairs):
-        for extra in (False, True):
-            finish(projected_at(step), extra)
+    finish(projected_at(2), True)
+    for extra in (False, True):
+        finish(projected_at(3), extra)
 
     with jax.named_scope("sends2"):
         others = weights.at[:, pl.ds(0, pairs - 1), core]

time: 109 us -> 107 us (0.982)
  Pallas kernels: 107 us -> 105 us
    pallas_call x1, Pallas kernels: 107 us -> 105 us  [exchanged_heads(): pl.pallas_call(functools.partial(exchange_kernel, pairs, groups, chunks),...]
where the time goes in v5:
time: 107 us; the launch traced here: 105 us
  Pallas kernels  105 us (98%)
    pallas_call x1, Pallas kernels, exchanged_heads(): pl.pallas_call(functools.partial(exchange_kernel, pairs, groups, chunks),...  105 us

profile of v5, /device:TPU:0, one launch (start us, length us, event | category | flops | bytes accessed | tf_op | source)
XLA Modules:
  0.0 105.5 jit_solution(6171933450713055327)
XLA Ops:
  0.0 104.7 %shard_map.82 = bf16[64,3072]{1,0:T(8,128)(2,1)S(1)} custom-call(bf16[256,3072]{1,0:T(8,128)(2,1)} %tokens.1, f32[1,3072]{1,0:T(1,128)} %bitcast.3, bf16[384,1024]{1,0:T(8,128)(2,1)} %q_w.1, bf16[384,1024]{1,0:T(8,128)(2,1)} %k_w.1, bf16[384,1024]{1,0:T(8,128)(2,1)} %v_w.1, f32[4,1,256]{2,1,0:T(1,128)} %bitcast.4, f32[4,1,256]{2,1,0:T(1,128)} %bitcast.5, ...), custom_call_target="tpu_custom_call" | custom-call | tf_op jit(solution)/shard_map/pallas_call | solution.py:800
  104.7 0.7 copy.10

commit v6 on v5

--- a/solution.py
+++ b/solution.py
@@ -91,8 +91,8 @@
 
 
 def exchange_kernel(
-    pairs, groups, chunks, tokens, ln_gain, q_w, k_w, v_w, q_gain, k_gain, out_w, result,
-    raw, normed, weights, own_rows, out_rows, end_rows, staged, context, kept, partial, arrived, summed, final,
+    pairs, groups, chunks, tokens, ln_gain_in, q_w, k_w, v_w, q_gain_in, k_gain_in, out_w, result,
+    ln_gain, head_gain, raw, normed, weights, own_rows, out_rows, end_rows, staged, context, kept, partial, arrived, summed, final,
     local_sem, token_send, token_recv, peer_send, first_recv, peer_recv,
     w_send, w_recv, own_send, own_recv, pass_send, pass_recv, out_send, out_recv, side_send, side_recv,
     end_send, end_recv, x_send, x_recv, c_send, c_recv, p_send, p_recv, f_send, f_recv,
@@ -132,6 +132,10 @@
     def quarter_of(owner):
         return pl.ds(pl.multiple_of(owner * part, part), part)
 
+    gain_copy = pltpu.make_async_copy(ln_gain_in, ln_gain, local_sem.at[groups + 2])
+    gain_copy.start()
+    for at, gain in enumerate((q_gain_in, k_gain_in)):
+        pltpu.make_async_copy(gain.at[pair], head_gain.at[at], local_sem.at[groups + 3]).start()
     token_quarters = []
     for j in range(groups):
         place = quarter_of((group + j) % groups)
@@ -188,8 +192,9 @@
             scaled = centred * lax.rsqrt(variance + epsilon) * ln_gain[...]
             normed[pair, place, :] = scaled.astype(jnp.bfloat16)
 
+    gain_copy.wait()
     token_quarters[0].wait()
-    normalise(group * part, part)
+    normalise(group * part, piece_rows)
 
     def piece(block, owner, k):
         start = pl.multiple_of(owner * part + k * piece_rows, 16)
@@ -255,7 +260,7 @@
     def rows_aside(side, k, device):
         return remote(
             side_of(out_rows, 0, side, k), side_of(out_rows, 1, side, k),
-            side_send, side_recv.at[side, k], device,
+            side_send, side_recv, device,
         )
 
     with jax.named_scope("greet"):
@@ -263,6 +268,10 @@
 
     @pl.loop(0, chunks)
     def _(k):
+        @pl.when(k > 0)
+        def _():
+            normalise(group * part + k * piece_rows, piece_rows)
+
         @pl.when(has_up)
         def _():
             z_hop(pair, k, True).start()
@@ -284,7 +293,7 @@
     def end_part(side, k, device):
         return remote(
             side_of(end_rows, 0, side, k), side_of(end_rows, 1, side, k),
-            end_send.at[2], end_recv.at[2 + 2 * side + k], device,
+            end_send.at[2], end_recv.at[2], device,
         )
 
     for at, up in ((0, True), (pairs - 1, False)):
@@ -298,6 +307,7 @@
             own_weight(h, t).start()
     for j in range(1, groups):
         token_quarters[j].wait()
+    pltpu.make_async_copy(head_gain, head_gain, local_sem.at[groups + 3]).wait()
 
     def relay(block, k, up):
         with jax.named_scope("relaywait"):
@@ -487,8 +497,8 @@
                 normed[image], weights[h].reshape(pairs * span, 3 * HEAD_DIM),
                 preferred_element_type=jnp.float32,
             )
-            queries = head_layer_norm(total[:, :HEAD_DIM], q_gain[pair, :, lanes])
-            key_rows = head_layer_norm(total[:, HEAD_DIM : 2 * HEAD_DIM], k_gain[pair, :, lanes])
+            queries = head_layer_norm(total[:, :HEAD_DIM], head_gain[0, :, lanes])
+            key_rows = head_layer_norm(total[:, HEAD_DIM : 2 * HEAD_DIM], head_gain[1, :, lanes])
             value_rows = total[:, 2 * HEAD_DIM :].astype(jnp.bfloat16)
             scores = lax.dot_general(
                 queries, key_rows, (((1,), (1,)), ((), ())), preferred_element_type=jnp.float32
@@ -613,7 +623,7 @@
 
     for step in range(pairs):
         half_in(image_at(step), 0)
-        send_context(image_at(step), 0, at_end | (step < 3), True)
+        send_context(image_at(step), 0, True, True)
     pass_weights(heads - 1)
     all_weights(heads - 1)
 
@@ -635,6 +645,10 @@
         def _():
             attend_head(image_at(step), heads - 1)
 
+        @pl.when(step == 0)
+        def _():
+            cross_context(image_at(0), 0)
+
         @pl.when((step > 0) & (step <= pairs))
         def _():
             image = image_at(step - 1)
@@ -643,11 +657,7 @@
 
             @pl.when(step < pairs)
             def _():
-                cross_context(image, 0)
-
-            @pl.when((step == 1) & ~at_end)
-            def _():
-                send_context(image_at(pairs - 1), 0, True, False)
+                cross_context(image_at(step), 0)
 
             for at, (turn, h, distance) in enumerate(((0, 0, 1), (1, 0, 1), (0, 0, 2))):
                 @pl.when((step == at + 1) & beside_end)
@@ -684,15 +694,10 @@
                 pass_context(image_at(1), 0, 2)
                 cross_context(image_at(2), heads - 1)
                 send_context(image_at(3), heads - 1, True, False)
-                cross_context(image_at(3), 0)
 
             @pl.when(step == lag + 1)
             def _():
                 cross_context(image_at(pairs - 1), heads - 1)
-
-            @pl.when(step == lag + 3)
-            def _():
-                finish(projected_at(2), False)
 
             pass_rest(image)
 
@@ -700,9 +705,8 @@
             def _():
                 @pl.when(step == lag)
                 def _():
-                    for side in range(2):
-                        for k in range(2):
-                            rows_aside(side, k, partner).wait_recv()
+                    whole = out_rows.at[1]
+                    remote(whole, whole, side_send, side_recv, partner).wait_recv()
 
                 project(image, image, out_rows)
 
@@ -712,15 +716,14 @@
                 def _():
                     end_pass(1 - core).wait_recv()
                     with jax.named_scope("endrows"):
-                        for side in range(2):
-                            for k in range(2):
-                                end_part(side, k, partner).wait_recv()
+                        whole = end_rows.at[1]
+                        remote(whole, whole, end_send.at[2], end_recv.at[2], partner).wait_recv()
 
                 project(pairs + image - 1, image, end_rows)
 
-    finish(projected_at(2), True)
-    for extra in (False, True):
-        finish(projected_at(3), extra)
+    for turn in (2, 3):
+        for extra in (False, True):
+            finish(projected_at(turn), extra)
 
     with jax.named_scope("sends2"):
         others = weights.at[:, pl.ds(0, pairs - 1), core]
@@ -754,7 +757,7 @@
 
     with jax.named_scope("sends3"):
         both = out_rows.at[0]
-        remote(both, both, side_send, side_recv.at[0], partner).wait_send()
+        remote(both, both, side_send, side_recv, partner).wait_send()
         half = staged.at[:, :, pl.ds(0, 2 * part), :]
         remote(half, half, x_send, x_recv.at[0, 0], partner).wait_send()
         for few, units in ((at_end, 2), (beside_end, 2 * pairs - 2)):
@@ -800,9 +803,11 @@
     return pl.pallas_call(
         functools.partial(exchange_kernel, pairs, groups, chunks),
         out_shape=pltpu.VMEM((part, features), bf16),
-        in_specs=[in_hbm, in_vmem, in_hbm, in_hbm, in_hbm, in_vmem, in_vmem, in_hbm],
+        in_specs=[in_hbm] * 8,
         out_specs=in_vmem,
         scratch_shapes=[
+            pltpu.VMEM((1, features), jnp.float32),
+            pltpu.VMEM((2, 1, width), jnp.float32),
             pltpu.VMEM((rows, features), bf16),
             pltpu.VMEM((pairs, rows, features), bf16),
             pltpu.VMEM((heads, pairs, 2, shard, 3 * HEAD_DIM), bf16),
@@ -816,9 +821,9 @@
             pltpu.VMEM((units, 2, part, shard), bf16),
             pltpu.VMEM((units, 2, part, shard), bf16),
             pltpu.VMEM((pairs, 2, part, shard), bf16),
-            dma((groups + 2,)), dma((2,)), dma((pairs, chunks)), dma, dma((pairs, chunks)), dma((pairs, 2)),
-            dma, dma((pairs, heads, 3)), dma, dma, dma, dma((heads,)), dma, dma, dma, dma((2, 2)),
-            dma((3,)), dma((6,)), dma, dma((pairs, heads)), dma((2,)), dma((pairs, pairs, heads)),
+            dma((groups + 4,)), dma((2,)), dma((pairs, chunks)), dma, dma((pairs, chunks)), dma((pairs, 2)),
+            dma, dma((pairs, heads, 3)), dma, dma, dma, dma((heads,)), dma, dma, dma, dma,
+            dma((3,)), dma((3,)), dma, dma((pairs, heads)), dma((2,)), dma((pairs, pairs, heads)),
             dma, dma((units, 2)), dma, dma,
         ],
         compiler_params=pltpu.CompilerParams(

time: 107 us -> 105 us (0.981)
    pallas_call x1, Pallas kernels: 105 us -> 104 us  [exchanged_heads(): pl.pallas_call(functools.partial(exchange_kernel, pairs, groups, chunks),...]
where the time goes in v6:
time: 105 us; the launch traced here: 104 us
  Pallas kernels  104 us (99%)
    pallas_call x1, Pallas kernels, exchanged_heads(): pl.pallas_call(functools.partial(exchange_kernel, pairs, groups, chunks),...  104 us

profile of v6, /device:TPU:0, one launch (start us, length us, event | category | flops | bytes accessed | tf_op | source)
XLA Modules:
  0.0 104.3 jit_solution(7443142698436940400)
XLA Ops:
  0.0 103.5 %shard_map.82 = bf16[64,3072]{1,0:T(8,128)(2,1)S(1)} custom-call(bf16[256,3072]{1,0:T(8,128)(2,1)} %tokens.1, f32[1,3072]{1,0:T(1,128)} %bitcast.3, bf16[384,1024]{1,0:T(8,128)(2,1)} %q_w.1, bf16[384,1024]{1,0:T(8,128)(2,1)} %k_w.1, bf16[384,1024]{1,0:T(8,128)(2,1)} %v_w.1, f32[4,1,256]{2,1,0:T(1,128)} %bitcast.4, f32[4,1,256]{2,1,0:T(1,128)} %bitcast.5, ...), custom_call_target="tpu_custom_call" | custom-call | tf_op jit(solution)/shard_map/pallas_call | solution.py:803
  103.6 0.7 copy.10

commit v7 on v6

--- a/solution.py
+++ b/solution.py
@@ -92,7 +92,7 @@
 
 def exchange_kernel(
     pairs, groups, chunks, tokens, ln_gain_in, q_w, k_w, v_w, q_gain_in, k_gain_in, out_w, result,
-    ln_gain, head_gain, raw, normed, weights, own_rows, out_rows, end_rows, staged, context, kept, partial, arrived, summed, final,
+    ln_gain, head_gain, raw, normed, weights, own_rows, out_rows, end_rows, staged, context, kept, partial, arrived, summed,
     local_sem, token_send, token_recv, peer_send, first_recv, peer_recv,
     w_send, w_recv, own_send, own_recv, pass_send, pass_recv, out_send, out_recv, side_send, side_recv,
     end_send, end_recv, x_send, x_recv, c_send, c_recv, p_send, p_recv, f_send, f_recv,
@@ -132,6 +132,23 @@
     def quarter_of(owner):
         return pl.ds(pl.multiple_of(owner * part, part), part)
 
+    greeted = pltpu.get_barrier_semaphore()
+    for step in range(1, pairs):
+        pl.semaphore_signal(
+            greeted, inc=1, device_id=at_pair((pair + step) % pairs), device_id_type=MESH
+        )
+    for step in range(1, groups):
+        pl.semaphore_signal(
+            greeted, inc=1, device_id=at_group((group + step) % groups), device_id_type=MESH
+        )
+    pl.semaphore_signal(greeted, inc=1, device_id=partner, device_id_type=MESH)
+    beside = group + 1 - 2 * (group % 2)
+    across = (group + 2) % 4
+    pl.semaphore_signal(
+        greeted, inc=1,
+        device_id=(pair * 2 + 1 - core, jnp.where(core == 0, beside, across)), device_id_type=MESH,
+    )
+
     gain_copy = pltpu.make_async_copy(ln_gain_in, ln_gain, local_sem.at[groups + 2])
     gain_copy.start()
     for at, gain in enumerate((q_gain_in, k_gain_in)):
@@ -152,23 +169,6 @@
 
     def slot(h, block, side, t):
         return weights.at[h, block, side, :, pl.ds(t * HEAD_DIM, HEAD_DIM)]
-
-    greeted = pltpu.get_barrier_semaphore()
-    for step in range(1, pairs):
-        pl.semaphore_signal(
-            greeted, inc=1, device_id=at_pair((pair + step) % pairs), device_id_type=MESH
-        )
-    for step in range(1, groups):
-        pl.semaphore_signal(
-            greeted, inc=1, device_id=at_group((group + step) % groups), device_id_type=MESH
-        )
-    pl.semaphore_signal(greeted, inc=1, device_id=partner, device_id_type=MESH)
-    beside = group + 1 - 2 * (group % 2)
-    across = (group + 2) % 4
-    pl.semaphore_signal(
-        greeted, inc=1,
-        device_id=(pair * 2 + 1 - core, jnp.where(core == 0, beside, across)), device_id_type=MESH,
-    )
 
     locals_ = [pltpu.make_async_copy(out_w, own_rows, local_sem.at[groups])]
     for h in range(heads):
@@ -220,7 +220,7 @@
     def weight_to(other, h, t):
         return remote(
             columns(other, h, t), slot(h, pair, core, t),
-            w_send, w_recv.at[pair, h, t], at_pair(other),
+            w_send, w_recv.at[pair, t if h > 0 else 3], at_pair(other),
         )
 
     def send_weights(up, plan):
@@ -379,12 +379,12 @@
 
                 @pl.when(other >= 0 if up else other < pairs)
                 def _():
-                    for t in range(3):
-                        there = slot(h, other, core, t)
+                    pieces = [(slot(h, other, core, t), t) for t in range(3)]
+                    if h == 0:
+                        pieces = [(weights.at[h, other, core], 3)]
+                    for there, at in pieces:
                         with jax.named_scope("wwait"):
-                            remote(
-                                there, there, w_send, w_recv.at[other, h, t], partner
-                            ).wait_recv()
+                            remote(there, there, w_send, w_recv.at[other, at], partner).wait_recv()
                         remote(there, there, pass_send, pass_recv.at[h], partner).start()
 
     def all_passed(h):
@@ -573,11 +573,16 @@
             partial.at[unit, c], arrived.at[unit, c], p_send, p_recv.at[unit, c], at_group(second)
         )
 
+    def span_place(span_of, c):
+        return pl.ds(pl.multiple_of(span_of * span + c * shard, 128), shard)
+
     def final_to(unit, c, image, span_of):
-        return remote(summed.at[unit, c], final.at[span_of, c], f_send, f_recv, at_pair(image))
+        return remote(
+            summed.at[unit, c], result.at[:, span_place(span_of, c)], f_send, f_recv, at_pair(image)
+        )
 
     def finals(count):
-        there = final.at[pl.ds(0, count)]
+        there = summed.at[pl.ds(0, count)]
         return remote(there, there, f_send, f_recv, partner)
 
     def project(unit, image, rows_of):
@@ -607,7 +612,7 @@
 
         @pl.when(image == pair)
         def _():
-            final[span_of, c] = total
+            result[:, span_place(span_of, c)] = total
 
     def own_unit(image):
         return ~at_end | outside(image)
@@ -728,7 +733,7 @@
     with jax.named_scope("sends2"):
         others = weights.at[:, pl.ds(0, pairs - 1), core]
         remote(others, others, pass_send, pass_recv.at[0], partner).wait_send()
-        remote(others, others, w_send, w_recv.at[0, 0, 0], partner).wait_send()
+        remote(others, others, w_send, w_recv.at[0, 0], partner).wait_send()
 
         @pl.when(at_end)
         def _():
@@ -774,10 +779,6 @@
         @pl.when(~at_end)
         def _():
             finals(pairs - 2).wait_recv()
-    for p in range(pairs):
-        for c in range(2):
-            start = (2 * p + c) * shard
-            result[:, start : start + shard] = final[p, c]
     with jax.named_scope("sends4"):
         @pl.when(at_end)
         def _():
@@ -820,9 +821,8 @@
             pltpu.VMEM((units, 2, part, shard), bf16),
             pltpu.VMEM((units, 2, part, shard), bf16),
             pltpu.VMEM((units, 2, part, shard), bf16),
-            pltpu.VMEM((pairs, 2, part, shard), bf16),
             dma((groups + 4,)), dma((2,)), dma((pairs, chunks)), dma, dma((pairs, chunks)), dma((pairs, 2)),
-            dma, dma((pairs, heads, 3)), dma, dma, dma, dma((heads,)), dma, dma, dma, dma,
+            dma, dma((pairs, 4)), dma, dma, dma, dma((heads,)), dma, dma, dma, dma,
             dma((3,)), dma((3,)), dma, dma((pairs, heads)), dma((2,)), dma((pairs, pairs, heads)),
             dma, dma((units, 2)), dma, dma,
         ],

time: 105 us -> 105 us (level)
  no operation moved by 1% of the time
where the time goes in v7:
time: 105 us; the launch traced here: 104 us
  Pallas kernels  103 us (98%)
    pallas_call x1, Pallas kernels, exchanged_heads(): pl.pallas_call(functools.partial(exchange_kernel, pairs, groups, chunks),...  103 us

profile of v7, /device:TPU:0, one launch (start us, length us, event | category | flops | bytes accessed | tf_op | source)
XLA Modules:
  0.0 104.2 jit_solution(4026110642939665656)
XLA Ops:
  0.0 103.4 %shard_map.82 = bf16[64,3072]{1,0:T(8,128)(2,1)S(1)} custom-call(bf16[256,3072]{1,0:T(8,128)(2,1)} %tokens.1, f32[1,3072]{1,0:T(1,128)} %bitcast.3, bf16[384,1024]{1,0:T(8,128)(2,1)} %q_w.1, bf16[384,1024]{1,0:T(8,128)(2,1)} %k_w.1, bf16[384,1024]{1,0:T(8,128)(2,1)} %v_w.1, f32[4,1,256]{2,1,0:T(1,128)} %bitcast.4, f32[4,1,256]{2,1,0:T(1,128)} %bitcast.5, ...), custom_call_target="tpu_custom_call" | custom-call | tf_op jit(solution)/shard_map/pallas_call | solution.py:804
  103.4 0.7 copy.10

commit v8 on v7

--- a/solution.py
+++ b/solution.py
@@ -681,11 +681,6 @@
             def _():
                 cross_context(image_at(0), heads - 1)
 
-            @pl.when(step == lag + 3)
-            def _():
-                for early in range(2):
-                    finish(projected_at(early), False)
-
             @pl.when(at_end | (step > lag + 1))
             def _():
                 pass_most(image)
@@ -706,6 +701,10 @@
 
             pass_rest(image)
 
+            @pl.when(step == lag + 2)
+            def _():
+                finish(projected_at(0), False)
+
             @pl.when(own_unit(image))
             def _():
                 @pl.when(step == lag)
@@ -714,6 +713,10 @@
                     remote(whole, whole, side_send, side_recv, partner).wait_recv()
 
                 project(image, image, out_rows)
+
+            @pl.when(step == lag + 2)
+            def _():
+                finish(projected_at(1), False)
 
             @pl.when(extra_unit(image))
             def _():

time: 105 us -> 105 us (level)
  no operation moved by 1% of the time
where the time goes in v8:
time: 105 us; the launch traced here: 104 us
  Pallas kernels  103 us (98%)
    pallas_call x1, Pallas kernels, exchanged_heads(): pl.pallas_call(functools.partial(exchange_kernel, pairs, groups, chunks),...  103 us

profile of v8, /device:TPU:0, one launch (start us, length us, event | category | flops | bytes accessed | tf_op | source)
XLA Modules:
  0.0 104.2 jit_solution(1058828352652306520)
XLA Ops:
  0.0 103.4 %shard_map.82 = bf16[64,3072]{1,0:T(8,128)(2,1)S(1)} custom-call(bf16[256,3072]{1,0:T(8,128)(2,1)} %tokens.1, f32[1,3072]{1,0:T(1,128)} %bitcast.3, bf16[384,1024]{1,0:T(8,128)(2,1)} %q_w.1, bf16[384,1024]{1,0:T(8,128)(2,1)} %k_w.1, bf16[384,1024]{1,0:T(8,128)(2,1)} %v_w.1, f32[4,1,256]{2,1,0:T(1,128)} %bitcast.4, f32[4,1,256]{2,1,0:T(1,128)} %bitcast.5, ...), custom_call_target="tpu_custom_call" | custom-call | tf_op jit(solution)/shard_map/pallas_call | solution.py:807
  103.4 0.7 copy.10

commit v9 on v8

--- a/solution.py
+++ b/solution.py
@@ -482,13 +482,13 @@
         return remote(
             staged.at[image, h, quarter_of(owner), :],
             context.at[image, 1, at, :, head_place(pair, h)],
-            x_send, x_recv.at[image, h], at_group(first),
+            x_send, x_recv.at[image if h > 0 else pairs], at_group(first),
         )
 
     def half_in(image, h):
         there = context.at[image, 1, :, :, head_place(pair, h)]
         with jax.named_scope("halfin"):
-            remote(there, there, x_send, x_recv.at[image, h], partner).wait_recv()
+            remote(there, there, x_send, x_recv.at[image], partner).wait_recv()
 
     def attend_head(image, h):
         lanes = slice(h * HEAD_DIM, (h + 1) * HEAD_DIM)
@@ -626,8 +626,9 @@
             for c in range(2):
                 add_up(pairs + image - 1 if extra else image, c, image, outer if extra else pair)
 
+    halves_in = context.at[:, 1, :, :, head_place(pair, 0)]
+    remote(halves_in, halves_in, x_send, x_recv.at[pairs], partner).wait_recv()
     for step in range(pairs):
-        half_in(image_at(step), 0)
         send_context(image_at(step), 0, True, True)
     pass_weights(heads - 1)
     all_weights(heads - 1)
@@ -767,7 +768,7 @@
         both = out_rows.at[0]
         remote(both, both, side_send, side_recv, partner).wait_send()
         half = staged.at[:, :, pl.ds(0, 2 * part), :]
-        remote(half, half, x_send, x_recv.at[0, 0], partner).wait_send()
+        remote(half, half, x_send, x_recv.at[0], partner).wait_send()
         for few, units in ((at_end, 2), (beside_end, 2 * pairs - 2)):
             @pl.when(few)
             def _():
@@ -826,7 +827,7 @@
             pltpu.VMEM((units, 2, part, shard), bf16),
             dma((groups + 4,)), dma((2,)), dma((pairs, chunks)), dma, dma((pairs, chunks)), dma((pairs, 2)),
             dma, dma((pairs, 4)), dma, dma, dma, dma((heads,)), dma, dma, dma, dma,
-            dma((3,)), dma((3,)), dma, dma((pairs, heads)), dma((2,)), dma((pairs, pairs, heads)),
+            dma((3,)), dma((3,)), dma, dma((pairs + 1,)), dma((2,)), dma((pairs, pairs, heads)),
             dma, dma((units, 2)), dma, dma,
         ],
         compiler_params=pltpu.CompilerParams(

time: 105 us -> 105 us (level)
  no operation moved by 1% of the time
where the time goes in v9:
time: 105 us; the launch traced here: 104 us
  Pallas kernels  103 us (98%)
    pallas_call x1, Pallas kernels, exchanged_heads(): pl.pallas_call(functools.partial(exchange_kernel, pairs, groups, chunks),...  103 us

profile of v9, /device:TPU:0, one launch (start us, length us, event | category | flops | bytes accessed | tf_op | source)
XLA Modules:
  0.0 104.2 jit_solution(16439433859613293294)
XLA Ops:
  0.0 103.4 %shard_map.82 = bf16[64,3072]{1,0:T(8,128)(2,1)S(1)} custom-call(bf16[256,3072]{1,0:T(8,128)(2,1)} %tokens.1, f32[1,3072]{1,0:T(1,128)} %bitcast.3, bf16[384,1024]{1,0:T(8,128)(2,1)} %q_w.1, bf16[384,1024]{1,0:T(8,128)(2,1)} %k_w.1, bf16[384,1024]{1,0:T(8,128)(2,1)} %v_w.1, f32[4,1,256]{2,1,0:T(1,128)} %bitcast.4, f32[4,1,256]{2,1,0:T(1,128)} %bitcast.5, ...), custom_call_target="tpu_custom_call" | custom-call | tf_op jit(solution)/shard_map/pallas_call | solution.py:808
  103.4 0.7 copy.10
